TPU v7x, 1024 devices: a whole 4x8x16 slice. The times are simulated.
1024 devices in a mesh: row: 8 (over z_lo), col: 128 (over x, z_hi, y, core).
Axes of the slice: x: 4, y: 8, z: 16 (z_hi: 2, z_lo: 8; z = z_hi * 8 + z_lo), core: 2. Of those that a mesh axis runs over, the one named last changes fastest.
Arguments:
- trailing: bfloat16 [8192, 65536], P('row', 'col'), may hold values from -12 to 12
- panel_left: bfloat16 [8192, 1024], P(('row', 'col')), may hold values from -1.5 to 1.5
- panel_right: bfloat16 [65536, 1024], P(('col', 'row')), may hold values from -1.5 to 1.5
- inverse_factors: float32 [2, 512, 512], replicated, may hold values from -2 to 2, as said below
- active: int32 [16, 128], P('row', 'col'), may hold values 0 or 1
Outputs:
- updated: bfloat16 [8192, 65536], P('row', 'col')
Inputs may be any that keep to these rules, and one draw needn't show every extreme that they name: `inverse_factors`: lower triangular, positive diagonal.
All inputs are finite; a program needn't handle non-finite values. No bound on the sum of `active` on one device may be relied on, other than what follows from the above.
Results may differ from a plain program's by a relative error of at most 0.0052.
Values may be sent and summed in bfloat16 or wider, within the bound.
No kernel may reach another device: no remote copies, remote signals or barrier semaphores. Data moves between devices by JAX's collectives and lax.ppermute only.
A program may use at most 32 MiB of HBM per device.

v0:
```python
import jax
import jax.numpy as jnp
from jax import lax
from jax.sharding import PartitionSpec as P


def triangle(rows, inverse_factors):
    width = inverse_factors.shape[1]
    parts = []
    for panel in range(inverse_factors.shape[0]):
        block = rows[:, panel * width : (panel + 1) * width].astype(jnp.float32)
        parts.append(
            jnp.dot(
                block,
                inverse_factors[panel].T,
                precision=lax.Precision.HIGHEST,
                preferred_element_type=jnp.float32,
            )
        )
    return jnp.concatenate(parts, axis=1).astype(jnp.bfloat16)


def outer_rows(piece, gathered):
    return lax.dot_general(
        piece, gathered, (((1,), (1,)), ((), ())), preferred_element_type=jnp.float32
    )


def local(trailing, panel_left, panel_right, inverse_factors, active):
    width = inverse_factors.shape[1]
    factor_left = triangle(panel_left, inverse_factors)
    factor_right = triangle(panel_right, inverse_factors)
    right_all = lax.all_gather(factor_right, "row", axis=0, tiled=True)
    change = outer_rows(lax.all_gather(factor_left, "col", axis=0, tiled=True), right_all)
    tile_rows = active.shape[0]
    tile_cols = active.shape[1]
    shaped = trailing.astype(jnp.float32).reshape(tile_rows, width, tile_cols, width)
    fresh = shaped - change.reshape(tile_rows, width, tile_cols, width)
    keep = active[:, None, :, None] == 1
    result = jnp.where(keep, fresh, shaped).astype(jnp.bfloat16)
    return result.reshape(trailing.shape)


def solution(mesh):
    in_specs = (
        P("row", "col"),
        P(("row", "col"), None),
        P(("col", "row"), None),
        P(),
        P("row", "col"),
    )
    out_specs = P("row", "col")
    return jax.shard_map(local, mesh=mesh, in_specs=in_specs, out_specs=out_specs, check_vma=False)
```

profile of v0, /device:TPU:1, one launch (start us, length us, event | category | flops | bytes accessed | tf_op | source)
XLA Modules:
  0.0 265.9 jit_solution(1586486713479752022)
XLA Ops:
  6.5 0.0 copy-start
  6.5 0.0 copy-start.1
  6.5 0.0 all-gather.5.cloned.1.call-start
  6.5 2.1 convolution_convert_fusion
  8.6 0.0 copy-start.3
  8.6 0.0 copy-start.2
  8.6 2.0 convolution_convert_fusion.1
  10.6 0.7 pad_maximum_fusion
  11.3 0.0 all-gather.5.cloned.1.call-update
  11.3 0.0 all-gather.3.cloned.1.call-start
  11.4 0.0 copy-done
  11.4 0.0 copy-done.1
  11.4 0.6 convolution_convert_fusion.2
  12.0 0.6 convolution_convert_fusion.3
  12.6 0.6 pad_maximum_fusion.1
  13.2 0.0 all-gather.3.cloned.1.call-update
  13.2 0.0 copy-done.3
  13.2 0.1 broadcast_in_dim.13
  13.3 70.9 %all-gather.5.cloned.1.call-done = bf16[512,1024]{1,0:T(8,128)(2,1)} async-done(((bf16[64,1024]{1,0:T(8,128)(2,1)}), bf16[512,1024]{1,0:T(8,128)(2,1)}) %all-gather.5.cloned.1.call-update) | async-done | bytes 1048592 | tf_op jit(solution)/shard_map/all_gather | solution.py:33
  84.3 170.6 %all-gather.3.cloned.1.call-done = bf16[1024,1024]{1,0:T(8,128)(2,1)} async-done(((bf16[8,1024]{1,0:T(8,128)(2,1)}), bf16[1024,1024]{1,0:T(8,128)(2,1)}) %all-gather.3.cloned.1.call-update) | async-done | bytes 2097168 | tf_op jit(solution)/shard_map/all_gather | solution.py:34
  254.9 0.0 copy-done.2
  254.9 4.1 %fusion = bf16[1024,512]{1,0:T(8,128)(2,1)} fusion(bf16[1024,512]{1,0:T(8,128)(2,1)S(1)} %copy-done.2, bf16[1024,1024]{1,0:T(8,128)(2,1)} %all-gather.3.cloned.1.call-done, bf16[512,1024]{1,0:T(8,128)(2,1)} %all-gather.5.cloned.1.call-done, pred[1024]{0:T(1024)(128)(4,1)S(1)} %broadcast_in_dim.14), kind=kOutput, calls=%fused_computation.1 | convolution fusion | flops 1075838976 | bytes 5243904 | tf_op jit(solution)/shard_map/dot_general | solution.py:24
  (2 shorter events, 0.0 us)
Async XLA Ops:
  6.5 4.8 %copy-start = (f32[2,512,512]{2,1,0:T(8,128)S(1)}, f32[2,512,512]{2,1,0:T(8,128)}, u32[]{:S(2)}) copy-start(f32[2,512,512]{2,1,0:T(8,128)} %param.8) | copy-start | bytes 6291460
  6.5 4.9 %copy-start.1 = (bf16[8,1024]{1,0:T(8,128)(2,1)S(1)}, bf16[8,1024]{1,0:T(8,128)(2,1)}, u32[]{:S(2)}) copy-start(bf16[8,1024]{1,0:T(8,128)(2,1)} %param.6) | copy-start | bytes 49156
  6.5 77.7 %all-gather.5.cloned.1.call-start = ((), (), s32[]{:S(2)}) async-start(), calls=%async_computation.1 | async-start | bytes 1179648 | tf_op jit(solution)/shard_map/all_gather | solution.py:33
  8.6 4.6 %copy-start.3 = (s32[2,1]{0,1:T(1,128)S(1)}, s32[2,1]{0,1:T(1,128)}, u32[]{:S(2)}) copy-start(s32[2,1]{0,1:T(1,128)} %param.9) | copy-start | bytes 28
  8.6 246.3 %copy-start.2 = (bf16[1024,512]{1,0:T(8,128)(2,1)S(1)}, bf16[1024,512]{1,0:T(8,128)(2,1)}, u32[]{:S(2)}) copy-start(bf16[1024,512]{1,0:T(8,128)(2,1)} %param.5) | copy-start | bytes 3145732
  11.3 243.6 %all-gather.3.cloned.1.call-start = ((), (), s32[]{:S(2)}) async-start(), calls=%async_computation | async-start | bytes 2113536 | tf_op jit(solution)/shard_map/all_gather | solution.py:34
Sparse Core Ops, SparseCore 0:
  11.4 72.7 all-gather.4
  90.1 164.7 all-gather.2
where the time goes:
time: 266 us
  waiting for transfers between devices  242 us (91%)
  between operations  13.5 us (5%)
  matrix products  9.36 us (4%)
    all_gather x1, waiting for transfers between devices, local(): lax.all_gather(factor_left, 'col', axis=0, tiled=True)  171 us
    all_gather x1, waiting for transfers between devices, local(): right_all = lax.all_gather(factor_right, 'row', axis=0, tiled=True)  70.9 us
  transfers between devices with their start and end apart: 2, of which 2 were waited for; matrix products, arithmetic and copies ran while one was open for 1% of the time, Pallas kernels for 0%

commit v1 on v0

v1 whole, which is shorter than its diff:
```python
import functools

import jax
import jax.numpy as jnp
from jax import lax
from jax.experimental import pallas as pl
from jax.experimental.pallas import tpu as pltpu
from jax.sharding import Mesh, PartitionSpec as P


VMEM = pl.BlockSpec(memory_space=pltpu.VMEM)
SMEM = pl.BlockSpec(memory_space=pltpu.SMEM)
SMALL = pltpu.CompilerParams(vmem_limit_bytes=16 * 2**20)


def factor_rows(rows, inverse_ref, store):
    panels, width, _ = inverse_ref.shape
    half = width // 2
    for panel in range(panels):
        for at in range(2):
            depth = (at + 1) * half
            block = rows[:, panel * width : panel * width + depth]
            exact = inverse_ref[panel, at * half : (at + 1) * half, :depth]
            high = exact.astype(jnp.bfloat16)
            rest = exact - high.astype(jnp.float32)
            middle = rest.astype(jnp.bfloat16)
            low = (rest - middle.astype(jnp.float32)).astype(jnp.bfloat16)
            total = None
            for part in (low, middle, high):
                term = lax.dot_general(
                    block, part, (((1,), (1,)), ((), ())), preferred_element_type=jnp.float32
                )
                total = term if total is None else total + term
            store(panel * width + at * half, total.astype(jnp.bfloat16))


def right_kernel(first_ref, second_ref, inverse_ref, out_ref):
    half = inverse_ref.shape[1] // 2

    def store(start, values):
        out_ref[:, start : start + half] = values

    rows = jnp.concatenate([first_ref[...], second_ref[...]], axis=0)
    factor_rows(rows, inverse_ref, store)


def left_kernel(core_ref, near_ref, inverse_ref, out_ref):
    half = inverse_ref.shape[1] // 2

    def store(start, values):
        out_ref[:, start : start + half] = values

    factor_rows(near_ref[core_ref[0]], inverse_ref, store)


def factor_cost(count, inverse):
    return pl.CostEstimate(
        flops=6 * count * inverse.shape[0] * inverse.shape[1] ** 2,
        bytes_accessed=inverse.size * 4 + 4 * count * inverse.shape[0] * inverse.shape[1],
        transcendentals=0,
    )


def factor_right(first, second, inverse):
    count = 2 * first.shape[0]
    return pl.pallas_call(
        right_kernel,
        out_shape=jax.ShapeDtypeStruct((count, first.shape[1]), jnp.bfloat16),
        in_specs=[VMEM, VMEM, VMEM],
        out_specs=VMEM,
        cost_estimate=factor_cost(count, inverse),
        compiler_params=SMALL,
        name="factor_right",
    )(first, second, inverse)


def factor_left(core, near, inverse):
    count = near.shape[1]
    return pl.pallas_call(
        left_kernel,
        out_shape=jax.ShapeDtypeStruct((count, near.shape[2]), jnp.bfloat16),
        in_specs=[SMEM, VMEM, VMEM],
        out_specs=VMEM,
        cost_estimate=factor_cost(count, inverse),
        compiler_params=SMALL,
        name="factor_left",
    )(core, near, inverse)


SLOTS = ((0, 4, 2, 6), (1, 5, 3, 7))


def update_kernel(where_ref, active_ref, left_ref, *refs, final):
    if final:
        right_ref, trailing_ref, _, out_ref = refs
        right = right_ref
    else:
        near_ref, far_ref, trailing_ref, out_ref, right = refs
        size = near_ref.shape[0] // 4

        @pl.when(pl.program_id(0) == 0)
        def _():
            for ref, slots in zip((near_ref, far_ref), SLOTS):
                for at, slot in enumerate(slots):
                    block = jnp.bitwise_xor(where_ref[1], slot)
                    right[pl.ds(pl.multiple_of(block * size, size), size), :] = ref[at * size : (at + 1) * size, :]

    x = pl.program_id(0)
    keep = active_ref[x // 2] == 1

    @pl.when(keep)
    def _():
        change = lax.dot_general(
            left_ref[x], right[...], (((1,), (1,)), ((), ())), preferred_element_type=jnp.float32
        )
        out_ref[0, 0] = (trailing_ref[0, 0].astype(jnp.float32) - change).astype(out_ref.dtype)

    @pl.when(jnp.logical_not(keep))
    def _():
        out_ref[0, 0] = trailing_ref[0, 0]


def update(where, active, left, rights, trailing, before=None):
    xs, _, rows, cols = trailing.shape
    features = left.shape[-1]
    picked = pl.BlockSpec((1, 1, rows, cols), lambda x, h, a: (x, h[0], 0, 0))
    final = before is not None
    in_specs = [VMEM] + [VMEM] * len(rights) + [picked]
    operands = [left, *rights, trailing]
    out_shape = [jax.ShapeDtypeStruct(trailing.shape, trailing.dtype)]
    out_specs = [picked]
    aliases = {}
    if final:
        in_specs.append(pl.BlockSpec(memory_space=pl.ANY))
        operands.append(before)
        aliases = {5: 0}
    else:
        out_shape.append(jax.ShapeDtypeStruct((cols, features), jnp.bfloat16))
        out_specs.append(VMEM)
    out = pl.pallas_call(
        functools.partial(update_kernel, final=final),
        out_shape=out_shape,
        grid_spec=pltpu.PrefetchScalarGridSpec(
            num_scalar_prefetch=2,
            grid=(xs,),
            in_specs=in_specs,
            out_specs=out_specs,
        ),
        input_output_aliases=aliases,
        cost_estimate=pl.CostEstimate(
            flops=2 * xs * rows * cols * features,
            bytes_accessed=4 * xs * rows * cols + 2 * cols * features + 2 * left.size,
            transcendentals=0,
        ),
        compiler_params=SMALL,
        name="update_second" if final else "update_first",
    )(where, active, *operands)
    return out


def spread(v, axes, n):
    return lax.all_to_all(jnp.broadcast_to(v[None], (n,) + v.shape), axes, 0, 0)


def swap(v, axis, bit, n):
    return lax.ppermute(v, axis, [(i, i ^ bit) for i in range(n)])


def local(trailing, panel_left, panel_right, inverse_factors, active):
    features = panel_left.shape[1]
    core = lax.axis_index("core").astype(jnp.int32)
    zlo = lax.axis_index("zlo").astype(jnp.int32)
    where = jnp.stack([core, zlo])
    near = spread(panel_left, ("zhi", "core"), 4).reshape(2, -1, features)
    across = swap(panel_right, "zlo", 4, 8)
    pair = factor_right(panel_right, across, inverse_factors)
    again = swap(pair, "zlo", 2, 8)
    quad = jnp.concatenate([pair, again], axis=0)
    far = swap(quad, "zlo", 1, 8)
    left = factor_left(where[:1], near, inverse_factors)
    own = spread(left, ("x", "y"), 32)
    other = swap(own, "core", 1, 2)
    flags = active.reshape(-1)
    view = trailing.reshape(4, 2, trailing.shape[0] // 8, trailing.shape[1])
    first, right = update(where, flags, own.reshape(4, -1, features), (quad, far), view)
    (second,) = update(
        jnp.stack([1 - core, zlo]), flags, other.reshape(4, -1, features), (right,), view, first
    )
    return second.reshape(trailing.shape)


def solution(mesh):
    fine = Mesh(mesh.devices.reshape(8, 4, 2, 8, 2), ("zlo", "x", "zhi", "y", "core"))
    col = ("x", "zhi", "y", "core")
    in_specs = (
        P("zlo", col),
        P(("zlo",) + col, None),
        P(col + ("zlo",), None),
        P(),
        P("zlo", col),
    )
    out_specs = P("zlo", col)
    return jax.shard_map(local, mesh=fine, in_specs=in_specs, out_specs=out_specs, check_vma=False)
```

time: 266 us -> 121 us (0.45)
  waiting for transfers between devices: 242 us -> 58.2 us
  starting transfers between devices: 0.04 us -> 47.4 us
  between operations: 13.5 us -> 0.11 us
  matrix products: 9.36 us -> 0 us
  Pallas kernels: 0 us -> 8.72 us
  local copies, waits for them, and re-layouts: 0.11 us -> 5.3 us
    all_gather x2 -> x0, waiting for transfers between devices: 242 us -> none  [the longest x1 171 us: local(): lax.all_gather(factor_left, 'col', axis=0, tiled=True)]
    all_to_all x0 -> x2, waiting for transfers between devices: none -> 32.3 us  [spread(): return lax.all_to_all(jnp.broadcast_to(v[None], (n,) + v.shape), axes, 0, 0)]
    all_to_all x0 -> x2, starting transfers between devices: none -> 29.9 us  [spread(): return lax.all_to_all(jnp.broadcast_to(v[None], (n,) + v.shape), axes, 0, 0)]
    ppermute x0 -> x4, waiting for transfers between devices: none -> 25.9 us  [swap(): return lax.ppermute(v, axis, [(i, i ^ bit) for i in range(n)])]
    ppermute x0 -> x4, starting transfers between devices: none -> 17.5 us  [swap(): return lax.ppermute(v, axis, [(i, i ^ bit) for i in range(n)])]
    dot_general x5 -> x0, matrix products: 9.36 us -> none  [the longest x4 5.24 us: triangle(): jnp.dot(block, inverse_factors[panel].T, precision=lax.Precision.HIGHEST,...]
    pallas_call x0 -> x4, Pallas kernels: none -> 8.72 us  [the longest x2 7.1 us: update(): pl.pallas_call(functools.partial(update_kernel, final=final), out_shape=o...]
    unnamed x8 -> x12, local copies, waits for them, and re-layouts: 0.02 us -> 2.85 us
  transfers between devices with their start and end apart: 2 -> 6, of which waited for: 2 -> 4; matrix products, arithmetic and copies ran while one was open for 1% -> 0% of each run, Pallas kernels for 0% -> 3%
where the time goes in v1:
time: 121 us; the launch traced here: 120 us
  waiting for transfers between devices  58.2 us (48%)
  starting transfers between devices  47.4 us (39%)
  Pallas kernels  8.72 us (7%)
  local copies, waits for them, and re-layouts  5.3 us (4%)
    all_to_all x2, waiting for transfers between devices, spread(): return lax.all_to_all(jnp.broadcast_to(v[None], (n,) + v.shape), axes, 0, 0)  32.3 us
    all_to_all x2, starting transfers between devices, spread(): return lax.all_to_all(jnp.broadcast_to(v[None], (n,) + v.shape), axes, 0, 0)  29.9 us
    ppermute x4, waiting for transfers between devices, swap(): return lax.ppermute(v, axis, [(i, i ^ bit) for i in range(n)])  25.9 us
    ppermute x4, starting transfers between devices, swap(): return lax.ppermute(v, axis, [(i, i ^ bit) for i in range(n)])  17.5 us
    pallas_call x2, Pallas kernels, update(): pl.pallas_call(functools.partial(update_kernel, final=final), out_shape=o...  7.1 us
    unnamed x12, local copies, waits for them, and re-layouts  2.85 us
    broadcast_in_dim x2, local copies, waits for them, and re-layouts, spread(): return lax.all_to_all(jnp.broadcast_to(v[None], (n,) + v.shape), axes, 0, 0)  2.45 us
  transfers between devices with their start and end apart: 6, of which 4 were waited for; matrix products, arithmetic and copies ran while one was open for 0% of the time, Pallas kernels for 3%

profile of v1, /device:TPU:1, one launch (start us, length us, event | category | flops | bytes accessed | tf_op | source)
XLA Modules:
  0.0 120.0 jit_solution(15042885854515734437)
XLA Ops:
  0.0 1.4 %broadcast_in_dim.4 = bf16[4,8,1024]{2,1,0:T(8,128)(2,1)} broadcast(bf16[8,1024]{1,0:T(8,128)(2,1)} %param.6), dimensions={1,2} | broadcast | bytes 81920 | tf_op jit(solution)/shard_map/broadcast_in_dim | solution.py:162
  1.4 20.2 %all-to-all-start = ((bf16[4,8,1024]{2,1,0:T(8,128)(2,1)}), bf16[4,8,1024]{2,1,0:T(8,128)(2,1)S(1)}, u32[]{:S(2)}, u32[]{:S(2)}) async-start(bf16[4,8,1024]{2,1,0:T(8,128)(2,1)} %broadcast_in_dim.4), calls=%async_computation | async-start | bytes 131072 | tf_op jit(solution)/shard_map/all_to_all | solution.py:162
  21.6 12.8 %all-to-all-done = bf16[4,8,1024]{2,1,0:T(8,128)(2,1)S(1)} async-done(((bf16[4,8,1024]{2,1,0:T(8,128)(2,1)}), bf16[4,8,1024]{2,1,0:T(8,128)(2,1)S(1)}, u32[]{:S(2)}, u32[]{:S(2)}) %all-to-all-start) | async-done | bytes 65568 | tf_op jit(solution)/shard_map/all_to_all | solution.py:162
  34.4 0.0 copy-start
  34.4 1.6 %copy-done = f32[2,512,512]{2,1,0:T(8,128)S(1)} copy-done((f32[2,512,512]{2,1,0:T(8,128)S(1)}, f32[2,512,512]{2,1,0:T(8,128)}, u32[]{:S(2)}) %copy-start) | copy-done | bytes 2097176
  36.0 0.7 factor_left.1
  36.7 0.0 copy-start.4
  36.7 0.0 copy-start.1
  36.7 1.1 broadcast_in_dim.5
  37.8 9.7 %all-to-all-start.1 = ((bf16[32,16,1024]{2,1,0:T(8,128)(2,1)}), bf16[32,16,1024]{2,1,0:T(8,128)(2,1)S(1)}, u32[]{:S(2)}, u32[]{:S(2)}) async-start(bf16[32,16,1024]{2,1,0:T(8,128)(2,1)} %broadcast_in_dim.5), calls=%async_computation.1 | async-start | bytes 2097152 | tf_op jit(solution)/shard_map/all_to_all | solution.py:162
  47.5 0.0 copy-done.4
  47.5 0.0 copy-start.5
  47.5 5.4 %collective-permute-start.1 = (bf16[64,1024]{1,0:T(8,128)(2,1)S(1)}, bf16[64,1024]{1,0:T(8,128)(2,1)S(1)}, u32[]{:S(2)}, u32[]{:S(2)}) collective-permute-start(bf16[64,1024]{1,0:T(8,128)(2,1)S(1)} %copy-done.4), channel_id=1, source_target_pairs={{0,512},{128,640},{256,768},{384,896},{512,0},{640,128},{768,256},... | collective-permute-start | bytes 393224 | tf_op jit(solution)/shard_map/ppermute | solution.py:166
  52.9 19.5 %all-to-all-done.1 = bf16[32,16,1024]{2,1,0:T(8,128)(2,1)S(1)} async-done(((bf16[32,16,1024]{2,1,0:T(8,128)(2,1)}), bf16[32,16,1024]{2,1,0:T(8,128)(2,1)S(1)}, u32[]{:S(2)}, u32[]{:S(2)}) %all-to-all-start.1) | async-done | bytes 1048608 | tf_op jit(solution)/shard_map/all_to_all | solution.py:162
  72.4 6.7 %collective-permute-start = (bf16[32,16,1024]{2,1,0:T(8,128)(2,1)S(1)}, bf16[32,16,1024]{2,1,0:T(8,128)(2,1)}, u32[]{:S(2)}, u32[]{:S(2)}) collective-permute-start(bf16[32,16,1024]{2,1,0:T(8,128)(2,1)S(1)} %all-to-all-done.1), channel_id=1, source_target_pairs={{0,1},{1,0},{2,3},{3,2},{4,5},{5,4},{6,7},{7,6},{8,9},{9,8},{10,11... | collective-permute-start | bytes 3145736 | tf_op jit(solution)/shard_map/ppermute | solution.py:166
  79.1 0.0 collective-permute-done.1.second_ref
  79.1 0.0 copy-done.1
  79.1 0.9 factor_right.1
  80.0 0.0 copy-start.3
  80.0 3.5 %collective-permute-start.2 = (bf16[128,1024]{1,0:T(8,128)(2,1)S(1)}, bf16[128,1024]{1,0:T(8,128)(2,1)S(1)}, u32[]{:S(2)}, u32[]{:S(2)}) collective-permute-start(bf16[128,1024]{1,0:T(8,128)(2,1)S(1)} %factor_right.1), channel_id=1, source_target_pairs={{0,256},{128,384},{256,0},{384,128},{512,768},{640,896},{768,512},... | collective-permute-start | bytes 786440 | tf_op jit(solution)/shard_map/ppermute | solution.py:166
  83.6 13.2 %collective-permute-done.2 = bf16[128,1024]{1,0:T(8,128)(2,1)S(1)} collective-permute-done((bf16[128,1024]{1,0:T(8,128)(2,1)S(1)}, bf16[128,1024]{1,0:T(8,128)(2,1)S(1)}, u32[]{:S(2)}, u32[]{:S(2)}) %collective-permute-start.2) | collective-permute-done | bytes 262176 | tf_op jit(solution)/shard_map/ppermute | solution.py:166
  96.8 1.9 %collective-permute-start.3 = (bf16[256,1024]{1,0:T(8,128)(2,1)S(1)}, bf16[256,1024]{1,0:T(8,128)(2,1)S(1)}, u32[]{:S(2)}, u32[]{:S(2)}) collective-permute-start(bf16[256,1024]{1,0:T(8,128)(2,1)S(1)} %pad_maximum_fusion.refs_0_), channel_id=1, source_target_pairs={{0,128},{128,0},{256,384},{384,256},{512,640},{640,512},{768,896},... | collective-permute-start | bytes 1572872 | tf_op jit(solution)/shard_map/ppermute | solution.py:166
  98.7 0.1 pad_add_fusion.1.where_ref
  98.8 0.1 pad_add_fusion.where_ref
  98.9 12.7 %collective-permute-done.3.refs_1_ = bf16[256,1024]{1,0:T(8,128)(2,1)S(1)} collective-permute-done((bf16[256,1024]{1,0:T(8,128)(2,1)S(1)}, bf16[256,1024]{1,0:T(8,128)(2,1)S(1)}, u32[]{:S(2)}, u32[]{:S(2)}) %collective-permute-start.3) | collective-permute-done | bytes 524320 | tf_op jit(solution)/shard_map/ppermute | solution.py:166
  111.6 0.0 copy-done.5
  111.6 0.0 copy-start.2
  111.6 1.2 %copy-done.2 = bf16[1024,512]{1,0:T(8,128)(2,1)S(1)} copy-done((bf16[1024,512]{1,0:T(8,128)(2,1)S(1)}, bf16[1024,512]{1,0:T(8,128)(2,1)}, u32[]{:S(2)}) %copy-start.2) | copy-done | bytes 1048600
  112.9 3.0 %update_first.1 = (bf16[4,2,128,512]{3,2,1,0:T(8,128)(2,1)}, bf16[512,1024]{1,0:T(8,128)(2,1)S(1)}) custom-call(s32[2]{0:T(128)S(1)} %pad_add_fusion.1.where_ref, s32[2]{0:T(128)S(1)} %bitcast.13, bf16[4,128,1024]{2,1,0:T(8,128)(2,1)S(1)} %bitcast.9, bf16[256,1024]{1,0:T(8,128)(2,1)S(1)} %pad_maximum_fusion.refs_0_, ...), custom_call_target="tpu_custom_call" | custom-call | flops 536870912 | bytes 3145728 | tf_op jit(solution)/shard_map/update_first/pallas_call | solution.py:140
  115.9 0.0 collective-permute-done
  115.9 0.0 copy-done.3
  115.9 4.1 %update_second.1 = bf16[4,2,128,512]{3,2,1,0:T(8,128)(2,1)} custom-call(s32[2]{0:T(128)S(1)} %pad_add_fusion.where_ref, s32[2]{0:T(128)S(1)} %bitcast.14, bf16[4,128,1024]{2,1,0:T(8,128)(2,1)} %bitcast.5.left_ref, bf16[512,1024]{1,0:T(8,128)(2,1)S(1)} %get-tuple-element.7.refs_0_, ...), custom_call_target="tpu_custom_call", output_to_operand_aliasing={{}: (5, {})} | custom-call | flops 536870912 | bytes 3145728 | tf_op jit(solution)/shard_map/update_second/pallas_call | solution.py:140
  (1 shorter events, 0.0 us)
Async XLA Ops:
  1.4 33.1 %all-to-all-start = ((bf16[4,8,1024]{2,1,0:T(8,128)(2,1)}), bf16[4,8,1024]{2,1,0:T(8,128)(2,1)S(1)}, u32[]{:S(2)}, u32[]{:S(2)}) async-start(bf16[4,8,1024]{2,1,0:T(8,128)(2,1)} %broadcast_in_dim.4), calls=%async_computation | async-start | bytes 131072 | tf_op jit(solution)/shard_map/all_to_all | solution.py:162
  34.4 1.6 %copy-start = (f32[2,512,512]{2,1,0:T(8,128)S(1)}, f32[2,512,512]{2,1,0:T(8,128)}, u32[]{:S(2)}) copy-start(f32[2,512,512]{2,1,0:T(8,128)} %inverse_ref.3) | copy-start | bytes 6291460
  36.7 10.8 %copy-start.4 = (bf16[64,1024]{1,0:T(8,128)(2,1)S(1)}, bf16[64,1024]{1,0:T(8,128)(2,1)}, u32[]{:S(2)}) copy-start(bf16[64,1024]{1,0:T(8,128)(2,1)} %first_ref.1) | copy-start | bytes 393220
  36.7 42.4 %copy-start.1 = (f32[2,512,512]{2,1,0:T(8,128)S(1)}, f32[2,512,512]{2,1,0:T(8,128)}, u32[]{:S(2)}) copy-start(f32[2,512,512]{2,1,0:T(8,128)} %inverse_ref.3) | copy-start | bytes 6291460
  37.8 34.5 %all-to-all-start.1 = ((bf16[32,16,1024]{2,1,0:T(8,128)(2,1)}), bf16[32,16,1024]{2,1,0:T(8,128)(2,1)S(1)}, u32[]{:S(2)}, u32[]{:S(2)}) async-start(bf16[32,16,1024]{2,1,0:T(8,128)(2,1)} %broadcast_in_dim.5), calls=%async_computation.1 | async-start | bytes 2097152 | tf_op jit(solution)/shard_map/all_to_all | solution.py:162
  47.5 64.1 %copy-start.5 = (s32[2,1]{0,1:T(1,128)S(1)}, s32[2,1]{0,1:T(1,128)}, u32[]{:S(2)}) copy-start(s32[2,1]{0,1:T(1,128)} %param.9) | copy-start | bytes 28
  47.5 31.6 %collective-permute-start.1 = (bf16[64,1024]{1,0:T(8,128)(2,1)S(1)}, bf16[64,1024]{1,0:T(8,128)(2,1)S(1)}, u32[]{:S(2)}, u32[]{:S(2)}) collective-permute-start(bf16[64,1024]{1,0:T(8,128)(2,1)S(1)} %copy-done.4), channel_id=1, source_target_pairs={{0,512},{128,640},{256,768},{384,896},{512,0},{640,128},{768,256},... | collective-permute-start | bytes 393224 | tf_op jit(solution)/shard_map/ppermute | solution.py:166
  72.4 43.5 %collective-permute-start = (bf16[32,16,1024]{2,1,0:T(8,128)(2,1)S(1)}, bf16[32,16,1024]{2,1,0:T(8,128)(2,1)}, u32[]{:S(2)}, u32[]{:S(2)}) collective-permute-start(bf16[32,16,1024]{2,1,0:T(8,128)(2,1)S(1)} %all-to-all-done.1), channel_id=1, source_target_pairs={{0,1},{1,0},{2,3},{3,2},{4,5},{5,4},{6,7},{7,6},{8,9},{9,8},{10,11... | collective-permute-start | bytes 3145736 | tf_op jit(solution)/shard_map/ppermute | solution.py:166
  80.0 35.8 %copy-start.3 = (bf16[1024,512]{1,0:T(8,128)(2,1)S(1)}, bf16[1024,512]{1,0:T(8,128)(2,1)}, u32[]{:S(2)}) copy-start(bf16[1024,512]{1,0:T(8,128)(2,1)} %param.5) | copy-start | bytes 3145732
  80.0 16.7 %collective-permute-start.2 = (bf16[128,1024]{1,0:T(8,128)(2,1)S(1)}, bf16[128,1024]{1,0:T(8,128)(2,1)S(1)}, u32[]{:S(2)}, u32[]{:S(2)}) collective-permute-start(bf16[128,1024]{1,0:T(8,128)(2,1)S(1)} %factor_right.1), channel_id=1, source_target_pairs={{0,256},{128,384},{256,0},{384,128},{512,768},{640,896},{768,512},... | collective-permute-start | bytes 786440 | tf_op jit(solution)/shard_map/ppermute | solution.py:166
  96.8 14.8 %collective-permute-start.3 = (bf16[256,1024]{1,0:T(8,128)(2,1)S(1)}, bf16[256,1024]{1,0:T(8,128)(2,1)S(1)}, u32[]{:S(2)}, u32[]{:S(2)}) collective-permute-start(bf16[256,1024]{1,0:T(8,128)(2,1)S(1)} %pad_maximum_fusion.refs_0_), channel_id=1, source_target_pairs={{0,128},{128,0},{256,384},{384,256},{512,640},{640,512},{768,896},... | collective-permute-start | bytes 1572872 | tf_op jit(solution)/shard_map/ppermute | solution.py:166
  111.6 1.2 %copy-start.2 = (bf16[1024,512]{1,0:T(8,128)(2,1)S(1)}, bf16[1024,512]{1,0:T(8,128)(2,1)}, u32[]{:S(2)}) copy-start(bf16[1024,512]{1,0:T(8,128)(2,1)} %param.5) | copy-start | bytes 3145732

commit v2 on v0

v2 whole, which is shorter than its diff:
```python
import jax
import jax.numpy as jnp
from jax import lax
from jax.experimental import pallas as pl
from jax.experimental.pallas import tpu as pltpu
from jax.sharding import Mesh, PartitionSpec as P


VMEM = pl.BlockSpec(memory_space=pltpu.VMEM)
SMEM = pl.BlockSpec(memory_space=pltpu.SMEM)
HBM = pl.BlockSpec(memory_space=pltpu.HBM)
ANY = pl.BlockSpec(memory_space=pl.ANY)
SMALL = pltpu.CompilerParams(vmem_limit_bytes=16 * 2**20)


def in_hbm(array):
    return pltpu.with_memory_space_constraint(array, pltpu.HBM)


def outer_rows(piece, gathered):
    return lax.dot_general(
        piece, gathered, (((1,), (1,)), ((), ())), preferred_element_type=jnp.float32
    )


def copy_all(copies):
    for copy in copies:
        copy.start()
    for copy in copies:
        copy.wait()


def spread_kernel(core_ref, near_ref, spread_hbm, sems):
    peers, few, _ = spread_hbm.shape
    mine = near_ref.at[pl.ds(pl.multiple_of(core_ref[0] * few, few), few)]
    copy_all([pltpu.make_async_copy(mine, spread_hbm.at[peer], sems.at[peer]) for peer in range(peers)])


def spread_rows(core, near, peers):
    return pl.pallas_call(
        spread_kernel,
        out_shape=pltpu.HBM((peers, near.shape[0] // 2, near.shape[1]), near.dtype),
        in_specs=[SMEM, VMEM],
        out_specs=HBM,
        scratch_shapes=[pltpu.SemaphoreType.DMA((peers,))],
        compiler_params=SMALL,
        cost_estimate=pl.CostEstimate(flops=0, bytes_accessed=16 * near.size, transcendentals=0),
        name="spread",
    )(core, near)


def join_kernel(first_any, second_any, out_ref, sems):
    count = first_any.shape[0]
    copy_all(
        [
            pltpu.make_async_copy(ref, out_ref.at[pl.ds(at * count, count)], sems.at[at])
            for at, ref in enumerate((first_any, second_any))
        ]
    )


def join(first, second):
    count, features = first.shape
    return pl.pallas_call(
        join_kernel,
        out_shape=pltpu.VMEM((2 * count, features), first.dtype),
        in_specs=[ANY, ANY],
        out_specs=VMEM,
        scratch_shapes=[pltpu.SemaphoreType.DMA((2,))],
        compiler_params=SMALL,
        cost_estimate=pl.CostEstimate(flops=0, bytes_accessed=8 * first.size, transcendentals=0),
        name="join",
    )(first, second)


def part_columns(at, half):
    return slice(at * half, (2 * at + 1) * half)


def split_kernel(inverse_hbm, parts_ref, inverse_ref, sems):
    panels, width, _ = inverse_hbm.shape
    half = width // 2
    steps = [(panel, at) for panel in range(panels) for at in range(2)]
    copies = []
    for panel, at in steps:
        place = (panel, pl.ds(at * half, half), pl.ds(0, (at + 1) * half))
        copies.append(pltpu.make_async_copy(inverse_hbm.at[place], inverse_ref.at[place], sems.at[panel, at]))
        copies[-1].start()
    for (panel, at), copy in zip(steps, copies):
        copy.wait()
        place = (panel, slice(at * half, (at + 1) * half), slice(0, (at + 1) * half))
        exact = inverse_ref[place]
        high = exact.astype(jnp.bfloat16)
        parts_ref[0, panel, :, part_columns(at, half)] = high
        parts_ref[1, panel, :, part_columns(at, half)] = (exact - high.astype(jnp.float32)).astype(jnp.bfloat16)


def split(inverse):
    panels, width, _ = inverse.shape
    return pl.pallas_call(
        split_kernel,
        out_shape=jax.ShapeDtypeStruct((2, panels, width // 2, 3 * width // 2), jnp.bfloat16),
        in_specs=[HBM],
        out_specs=VMEM,
        scratch_shapes=[pltpu.VMEM(inverse.shape, inverse.dtype), pltpu.SemaphoreType.DMA((inverse.shape[0], 2))],
        compiler_params=SMALL,
        cost_estimate=pl.CostEstimate(flops=4 * inverse.size, bytes_accessed=8 * inverse.size, transcendentals=0),
        name="split",
    )(in_hbm(inverse))


def factor_rows(rows_ref, parts_ref, store):
    _, panels, half, _ = parts_ref.shape
    width = 2 * half
    for panel in range(panels):
        for at in range(2):
            depth = (at + 1) * half
            rows = rows_ref[:, panel * width : panel * width + depth]
            high, rest = (parts_ref[term, panel, :, part_columns(at, half)] for term in range(2))
            total = outer_rows(rows, rest) + outer_rows(rows, high)
            start = panel * width + at * half
            store(slice(start, start + half), total.astype(jnp.bfloat16))


def factor_cost(rows, features, width, copies):
    return pl.CostEstimate(
        flops=4 * rows * features * width,
        bytes_accessed=4 * features * width + 2 * (1 + copies) * rows * features,
        transcendentals=0,
    )


def factor_left_kernel(rows_ref, parts_ref, spread_hbm, done_ref, sems):
    peers, count, _ = spread_hbm.shape
    copies = []

    def store(columns, values):
        done_ref[:, columns] = values
        place = (pl.ds(0, count), pl.ds(columns.start, columns.stop - columns.start))
        step = len(copies) // peers
        for peer in range(peers):
            copies.append(
                pltpu.make_async_copy(done_ref.at[place], spread_hbm.at[(peer,) + place], sems.at[step, peer])
            )
            copies[-1].start()

    factor_rows(rows_ref, parts_ref, store)
    for copy in copies:
        copy.wait()


def factor_left(rows, parts, peers):
    return pl.pallas_call(
        factor_left_kernel,
        out_shape=pltpu.HBM((peers,) + rows.shape, rows.dtype),
        in_specs=[VMEM, VMEM],
        out_specs=HBM,
        scratch_shapes=[pltpu.VMEM(rows.shape, rows.dtype), pltpu.SemaphoreType.DMA((4, peers))],
        compiler_params=SMALL,
        cost_estimate=factor_cost(*rows.shape, 2 * parts.shape[2], peers),
        name="factor_left" if peers > 1 else "factor_right",
    )(rows, parts)


PAIRS = ((0, 4), (2, 6), (1, 5), (3, 7))


def block_starts(zlo_ref, slots, size):
    return [pl.multiple_of(jnp.bitwise_xor(zlo_ref[0], slot) * size, size) for slot in slots]


def gathered_kernel(
    zlo_ref, own_hbm, across_hbm, third_hbm, second_hbm, last_hbm, parts_ref, right_ref, rows_ref, in_sems, out_sems
):
    size = own_hbm.shape[0]
    raw = [
        pltpu.make_async_copy(ref, rows_ref.at[pl.ds(at * size, ref.shape[0])], in_sems.at[at])
        for at, ref in enumerate((own_hbm, across_hbm, third_hbm))
    ]
    placed = []
    for pair, ref in ((1, second_hbm), (3, last_hbm)):
        for at, start in enumerate(block_starts(zlo_ref, PAIRS[pair], size)):
            place = right_ref.at[pl.ds(start, size)]
            placed.append(pltpu.make_async_copy(ref.at[pl.ds(at * size, size)], place, out_sems.at[pair // 2, at]))
    for copy in raw + placed:
        copy.start()
    starts = [start for pair in (0, 2) for start in block_starts(zlo_ref, PAIRS[pair], size)]

    def store(columns, values):
        for at, start in enumerate(starts):
            right_ref[pl.ds(start, size), columns] = values[at * size : (at + 1) * size]

    for copy in raw:
        copy.wait()
    factor_rows(rows_ref, parts_ref, store)
    for copy in placed:
        copy.wait()


def gathered(zlo, own, across, third, second, last, parts):
    size, features = own.shape
    return pl.pallas_call(
        gathered_kernel,
        out_shape=jax.ShapeDtypeStruct((8 * size, features), parts.dtype),
        in_specs=[SMEM, HBM, ANY, ANY, HBM, ANY, VMEM],
        out_specs=VMEM,
        scratch_shapes=[
            pltpu.VMEM((4 * size, features), parts.dtype),
            pltpu.SemaphoreType.DMA((3,)),
            pltpu.SemaphoreType.DMA((2, 2)),
        ],
        compiler_params=SMALL,
        cost_estimate=factor_cost(4 * size, features, 2 * parts.shape[2], 1),
        name="gathered",
    )(zlo, in_hbm(own), across, third, in_hbm(second), last, parts)


def change_tile(tile, tile_rows, active_ref, left_ref, right_ref, trailing_ref, done_ref):
    xs, rows, _ = done_ref.shape
    group = xs // tile_rows
    place = slice(tile * group, (tile + 1) * group)
    left = left_ref[place].reshape(group * rows, left_ref.shape[-1])
    change = outer_rows(left, right_ref[...])
    before = trailing_ref[place].astype(jnp.float32)
    fresh = before - change.reshape(before.shape)
    keep = active_ref[tile] == 1
    done_ref[place] = jnp.where(keep, fresh, before).astype(done_ref.dtype)


def tile_spans(xs, tile_rows):
    group = xs // tile_rows
    return [pl.ds(tile * group, group) for tile in range(tile_rows)]


def first_kernel(half_ref, active_ref, left_any, right_ref, trailing_hbm, done_ref, next_ref, left_ref, trailing_ref, sems):
    half = half_ref[0]
    tile_rows = active_ref.shape[0]
    xs = done_ref.shape[0]
    spans = tile_spans(xs, tile_rows)
    steps = []
    for tile, span in enumerate(spans):
        steps.append(
            (
                pltpu.make_async_copy(left_any.at[span], left_ref.at[span], sems.at[0, tile]),
                pltpu.make_async_copy(trailing_hbm.at[span, half], trailing_ref.at[span], sems.at[1, tile]),
            )
        )
        for copy in steps[-1]:
            copy.start()
    ahead = pltpu.make_async_copy(trailing_hbm.at[pl.ds(0, xs), 1 - half], next_ref, sems.at[2, 0])
    ahead.start()
    for tile, pair in enumerate(steps):
        for copy in pair:
            copy.wait()
        change_tile(tile, tile_rows, active_ref, left_ref, right_ref, trailing_ref, done_ref)
    ahead.wait()


def update_cost(left, right):
    rows = left.shape[0] * left.shape[1]
    return pl.CostEstimate(
        flops=2 * rows * right.size, bytes_accessed=2 * left.size + 2 * right.size + 4 * rows * right.shape[0],
        transcendentals=0,
    )


def update_first(half, active, left, right, trailing):
    shape = left.shape[:2] + trailing.shape[3:]
    return pl.pallas_call(
        first_kernel,
        out_shape=[jax.ShapeDtypeStruct(shape, trailing.dtype)] * 2,
        in_specs=[SMEM] * 2 + [ANY, VMEM, HBM],
        out_specs=[VMEM] * 2,
        scratch_shapes=[
            pltpu.VMEM(left.shape, left.dtype),
            pltpu.VMEM(shape, trailing.dtype),
            pltpu.SemaphoreType.DMA((3, active.shape[0])),
        ],
        compiler_params=SMALL,
        cost_estimate=update_cost(left, right),
        name="update_first",
    )(half, active, left, right, in_hbm(trailing))


def second_kernel(half_ref, active_ref, left_ref, right_ref, first_ref, trailing_ref, out_hbm, done_ref, sems):
    half = half_ref[0]
    tile_rows = active_ref.shape[0]
    xs = first_ref.shape[0]
    copies = [pltpu.make_async_copy(first_ref, out_hbm.at[pl.ds(0, xs), 1 - half], sems.at[tile_rows])]
    copies[0].start()
    for tile, span in enumerate(tile_spans(xs, tile_rows)):
        change_tile(tile, tile_rows, active_ref, left_ref, right_ref, trailing_ref, done_ref)
        copies.append(pltpu.make_async_copy(done_ref.at[span], out_hbm.at[span, half], sems.at[tile]))
        copies[-1].start()
    for copy in copies:
        copy.wait()


def update_second(half, active, left, right, first, held, shape):
    return pl.pallas_call(
        second_kernel,
        out_shape=pltpu.HBM(shape, first.dtype),
        in_specs=[SMEM] * 2 + [VMEM] * 4,
        out_specs=HBM,
        scratch_shapes=[
            pltpu.VMEM(first.shape, first.dtype),
            pltpu.SemaphoreType.DMA((active.shape[0] + 1,)),
        ],
        compiler_params=SMALL,
        cost_estimate=update_cost(left, right),
        name="update_second",
    )(half, active, left, right, first, held)


def swap(v, axis, bit, n):
    return lax.ppermute(v, axis, [(i, i ^ bit) for i in range(n)])


def local(trailing, panel_left, panel_right, inverse_factors, active):
    features = panel_left.shape[1]
    core = lax.axis_index("core").astype(jnp.int32).reshape(1)
    zlo = lax.axis_index("zlo").astype(jnp.int32).reshape(1)
    across = swap(panel_right, "zlo", 4, 8)
    near = lax.all_gather(panel_left, ("zhi", "core"), axis=0, tiled=True)
    spread = spread_rows(core, near, 8)
    pair = join(in_hbm(panel_right), across)
    line = lax.all_to_all(spread, "y", 0, 0).reshape(-1, features)
    parts = split(inverse_factors)
    second = swap(pair, "zlo", 2, 8)
    third = swap(pair, "zlo", 1, 8)
    wide = factor_left(line, parts, 4)
    own = lax.all_to_all(wide, "x", 0, 0)
    second = factor_left(second, parts, 1).reshape(second.shape)
    last = swap(second, "zlo", 1, 8)
    view = trailing.reshape(4, 2, trailing.shape[0] // 8, trailing.shape[1])
    right = gathered(zlo, panel_right, across, third, second, last, parts)
    other = swap(own, "core", 1, 2)
    flags = active.reshape(-1)
    first, held = update_first(core, flags, own, right, view)
    result = update_second(1 - core, flags, other, right, first, held, view.shape)
    return result.reshape(trailing.shape)


def solution(mesh):
    fine = Mesh(mesh.devices.reshape(8, 4, 2, 8, 2), ("zlo", "x", "zhi", "y", "core"))
    col = ("x", "zhi", "y", "core")
    in_specs = (
        P("zlo", col),
        P(("zlo",) + col, None),
        P(col + ("zlo",), None),
        P(),
        P("zlo", col),
    )
    out_specs = P("zlo", col)
    return jax.shard_map(local, mesh=fine, in_specs=in_specs, out_specs=out_specs, check_vma=False)
```

time: 266 us -> 120 us (0.45)
  waiting for transfers between devices: 242 us -> 43.3 us
  blocking collectives: 0 us -> 46.3 us
  starting transfers between devices: 0.04 us -> 16.4 us
  between operations: 13.5 us -> 0.15 us
  Pallas kernels: 0 us -> 13 us
  matrix products: 9.36 us -> 0 us
    all_gather x2 -> x0, waiting for transfers between devices: 242 us -> none  [the longest x1 171 us: local(): lax.all_gather(factor_left, 'col', axis=0, tiled=True)]
    ppermute x0 -> x5, waiting for transfers between devices: none -> 32.5 us  [swap(): return lax.ppermute(v, axis, [(i, i ^ bit) for i in range(n)])]
    all_gather x0 -> x1, blocking collectives: none -> 28.1 us  [local(): near = lax.all_gather(panel_left, ('zhi', 'core'), axis=0, tiled=True)]
    all_to_all x0 -> x1, blocking collectives: none -> 18.2 us  [local(): own = lax.all_to_all(wide, 'x', 0, 0)]
    pallas_call x0 -> x8, Pallas kernels: none -> 13 us  [the longest x2 2.99 us: factor_left(): pl.pallas_call(factor_left_kernel, out_shape=pltpu.HBM((peers,) + rows.sh...]
    ppermute x0 -> x5, starting transfers between devices: none -> 13 us  [swap(): return lax.ppermute(v, axis, [(i, i ^ bit) for i in range(n)])]
    all_to_all x0 -> x1, waiting for transfers between devices: none -> 10.8 us  [local(): line = lax.all_to_all(spread, 'y', 0, 0).reshape(-1, features)]
    dot_general x5 -> x0, matrix products: 9.36 us -> none  [the longest x4 5.24 us: triangle(): jnp.dot(block, inverse_factors[panel].T, precision=lax.Precision.HIGHEST,...]
  transfers between devices with their start and end apart: 2 -> 6, of which waited for: 2 -> 4; matrix products, arithmetic and copies ran while one was open for 1% -> 0% of each run, Pallas kernels for 0% -> 7%
where the time goes in v2:
time: 120 us; the launch traced here: 119 us
  blocking collectives  46.3 us (39%)
  waiting for transfers between devices  43.3 us (36%)
  starting transfers between devices  16.4 us (14%)
  Pallas kernels  13 us (11%)
    ppermute x5, waiting for transfers between devices, swap(): return lax.ppermute(v, axis, [(i, i ^ bit) for i in range(n)])  32.5 us
    all_gather x1, blocking collectives, local(): near = lax.all_gather(panel_left, ('zhi', 'core'), axis=0, tiled=True)  28.1 us
    all_to_all x1, blocking collectives, local(): own = lax.all_to_all(wide, 'x', 0, 0)  18.2 us
    ppermute x5, starting transfers between devices, swap(): return lax.ppermute(v, axis, [(i, i ^ bit) for i in range(n)])  13 us
    all_to_all x1, waiting for transfers between devices, local(): line = lax.all_to_all(spread, 'y', 0, 0).reshape(-1, features)  10.8 us
    all_to_all x1, starting transfers between devices, local(): line = lax.all_to_all(spread, 'y', 0, 0).reshape(-1, features)  3.42 us
    pallas_call x2, Pallas kernels, factor_left(): pl.pallas_call(factor_left_kernel, out_shape=pltpu.HBM((peers,) + rows.sh...  2.99 us
    pallas_call x1, Pallas kernels, update_second(): pl.pallas_call(second_kernel, out_shape=pltpu.HBM(shape, first.dtype), in...  2.72 us
  transfers between devices with their start and end apart: 6, of which 4 were waited for; matrix products, arithmetic and copies ran while one was open for 0% of the time, Pallas kernels for 7%

profile of v2, /device:TPU:1, one launch (start us, length us, event | category | flops | bytes accessed | tf_op | source)
XLA Modules:
  0.0 119.2 jit_solution(4322152441287532166)
XLA Ops:
  0.0 28.1 %all_gather.3.near_ref = bf16[32,1024]{1,0:T(8,128)(2,1)S(1)} all-gather(bf16[8,1024]{1,0:T(8,128)(2,1)} %param.6), channel_id=1, replica_groups=mesh['zlo'=8,'x'=4,'zhi'=2,'y'=8,'core'=2] {'zhi','core'}, dimensions={0}, use_global_device_ids=true | all-gather | bytes 81920 | tf_op jit(solution)/shard_map/all_gather | solution.py:324
  28.1 0.8 spread.1
  28.9 3.4 %all-to-all-start = ((bf16[8,16,1024]{2,1,0:T(8,128)(2,1)}), bf16[8,16,1024]{2,1,0:T(8,128)(2,1)S(1)}, u32[]{:S(2)}, u32[]{:S(2)}) async-start(bf16[8,16,1024]{2,1,0:T(8,128)(2,1)} %spread.1), calls=%async_computation | async-start | bytes 524288 | tf_op jit(solution)/shard_map/all_to_all | solution.py:327
  32.3 1.5 %split.1.parts_ref = bf16[2,2,256,768]{3,2,1,0:T(8,128)(2,1)S(1)} custom-call(f32[2,512,512]{2,1,0:T(8,128)} %inverse_hbm.1), custom_call_target="tpu_custom_call" | custom-call | flops 2097152 | bytes 4194304 | tf_op jit(solution)/shard_map/split/pallas_call | solution.py:100
  33.8 10.8 %all-to-all-done = bf16[8,16,1024]{2,1,0:T(8,128)(2,1)S(1)} async-done(((bf16[8,16,1024]{2,1,0:T(8,128)(2,1)}), bf16[8,16,1024]{2,1,0:T(8,128)(2,1)S(1)}, u32[]{:S(2)}, u32[]{:S(2)}) %all-to-all-start) | async-done | bytes 262176 | tf_op jit(solution)/shard_map/all_to_all | solution.py:327
  44.6 0.0 copy-start.1
  44.6 1.6 %factor_left.1 = bf16[4,128,1024]{2,1,0:T(8,128)(2,1)} custom-call(bf16[128,1024]{1,0:T(8,128)(2,1)S(1)} %bitcast.7, bf16[2,2,256,768]{3,2,1,0:T(8,128)(2,1)S(1)} %split.1.parts_ref), custom_call_target="tpu_custom_call" | custom-call | flops 268435456 | bytes 3407872 | tf_op jit(solution)/shard_map/factor_left/pallas_call | solution.py:153
  46.2 18.2 %all_to_all.10.left_any = bf16[4,128,1024]{2,1,0:T(8,128)(2,1)S(1)} all-to-all(bf16[4,128,1024]{2,1,0:T(8,128)(2,1)} %factor_left.1), channel_id=1, replica_groups=mesh['zlo'=8,'x'=4,'zhi'=2,'y'=8,'core'=2] {'x'}, dimensions={0} | all-to-all | bytes 2097152 | tf_op jit(solution)/shard_map/all_to_all | solution.py:332
  64.5 3.2 %collective-permute-start = (bf16[4,128,1024]{2,1,0:T(8,128)(2,1)S(1)}, bf16[4,128,1024]{2,1,0:T(8,128)(2,1)}, u32[]{:S(2)}, u32[]{:S(2)}) collective-permute-start(bf16[4,128,1024]{2,1,0:T(8,128)(2,1)S(1)} %all_to_all.10.left_any), channel_id=1, source_target_pairs={{0,1},{1,0},{2,3},{3,2},{4,5},{5,4},{6,7},{7,6},{8,9},{9,8},{10,11... | collective-permute-start | bytes 3145736 | tf_op jit(solution)/shard_map/ppermute | solution.py:316
  67.7 0.0 copy-done.1
  67.7 3.9 %collective-permute-start.1 = (bf16[64,1024]{1,0:T(8,128)(2,1)S(1)}, bf16[64,1024]{1,0:T(8,128)(2,1)S(1)}, u32[]{:S(2)}, u32[]{:S(2)}) collective-permute-start(bf16[64,1024]{1,0:T(8,128)(2,1)S(1)} %copy-done.1), channel_id=1, source_target_pairs={{0,512},{128,640},{256,768},{384,896},{512,0},{640,128},{768,256},... | collective-permute-start | bytes 393224 | tf_op jit(solution)/shard_map/ppermute | solution.py:316
  71.6 14.8 %collective-permute-done.1.second_any.across_hbm = bf16[64,1024]{1,0:T(8,128)(2,1)S(1)} collective-permute-done((bf16[64,1024]{1,0:T(8,128)(2,1)S(1)}, bf16[64,1024]{1,0:T(8,128)(2,1)S(1)}, u32[]{:S(2)}, u32[]{:S(2)}) %collective-permute-start.1) | collective-permute-done | bytes 131104 | tf_op jit(solution)/shard_map/ppermute | solution.py:316
  86.3 0.9 join.1
  87.3 1.9 %collective-permute-start.3 = (bf16[128,1024]{1,0:T(8,128)(2,1)S(1)}, bf16[128,1024]{1,0:T(8,128)(2,1)S(1)}, u32[]{:S(2)}, u32[]{:S(2)}) collective-permute-start(bf16[128,1024]{1,0:T(8,128)(2,1)S(1)} %join.1), channel_id=1, source_target_pairs={{0,256},{128,384},{256,0},{384,128},{512,768},{640,896},{768,512},... | collective-permute-start | bytes 786440 | tf_op jit(solution)/shard_map/ppermute | solution.py:316
  89.2 2.1 %collective-permute-start.2 = (bf16[128,1024]{1,0:T(8,128)(2,1)S(1)}, bf16[128,1024]{1,0:T(8,128)(2,1)S(1)}, u32[]{:S(2)}, u32[]{:S(2)}) collective-permute-start(bf16[128,1024]{1,0:T(8,128)(2,1)S(1)} %join.1), channel_id=1, source_target_pairs={{0,128},{128,0},{256,384},{384,256},{512,640},{640,512},{768,896},... | collective-permute-start | bytes 786440 | tf_op jit(solution)/shard_map/ppermute | solution.py:316
  91.3 10.2 %collective-permute-done.3.rows_ref = bf16[128,1024]{1,0:T(8,128)(2,1)S(1)} collective-permute-done((bf16[128,1024]{1,0:T(8,128)(2,1)S(1)}, bf16[128,1024]{1,0:T(8,128)(2,1)S(1)}, u32[]{:S(2)}, u32[]{:S(2)}) %collective-permute-start.3) | collective-permute-done | bytes 262176 | tf_op jit(solution)/shard_map/ppermute | solution.py:316
  101.5 1.4 %factor_right.1 = bf16[1,128,1024]{2,1,0:T(8,128)(2,1)} custom-call(bf16[128,1024]{1,0:T(8,128)(2,1)S(1)} %collective-permute-done.3.rows_ref, bf16[2,2,256,768]{3,2,1,0:T(8,128)(2,1)S(1)} %split.1.parts_ref), custom_call_target="tpu_custom_call" | custom-call | flops 268435456 | bytes 2621440 | tf_op jit(solution)/shard_map/factor_right/pallas_call | solution.py:153
  102.9 0.0 copy-start
  102.9 1.9 %collective-permute-start.4 = (bf16[128,1024]{1,0:T(8,128)(2,1)}, bf16[128,1024]{1,0:T(8,128)(2,1)S(1)}, u32[]{:S(2)}, u32[]{:S(2)}) collective-permute-start(bf16[128,1024]{1,0:T(8,128)(2,1)} %bitcast.11), channel_id=1, source_target_pairs={{0,128},{128,0},{256,384},{384,256},{512,640},{640,512},{768,896},... | collective-permute-start | bytes 786440 | tf_op jit(solution)/shard_map/ppermute | solution.py:316
  104.8 0.0 collective-permute-done.2.third_hbm
  104.8 7.5 %collective-permute-done.4.last_hbm = bf16[128,1024]{1,0:T(8,128)(2,1)S(1)} collective-permute-done((bf16[128,1024]{1,0:T(8,128)(2,1)}, bf16[128,1024]{1,0:T(8,128)(2,1)S(1)}, u32[]{:S(2)}, u32[]{:S(2)}) %collective-permute-start.4) | collective-permute-done | bytes 262176 | tf_op jit(solution)/shard_map/ppermute | solution.py:316
  112.3 1.6 %gathered.1.right_ref = bf16[512,1024]{1,0:T(8,128)(2,1)S(1)} custom-call(s32[1]{0:T(128)} %bitcast.3.zlo_ref, bf16[64,1024]{1,0:T(8,128)(2,1)} %own_hbm.1, bf16[64,1024]{1,0:T(8,128)(2,1)S(1)} %collective-permute-done.1.second_any.across_hbm, bf16[128,1024]{1,0:T(8,128)(2,1)S(1)} %collective-permute-done.2.third_hbm, bf16[128,1024]{1,0:T(8,128)(2,1)} %bitcast.12, ...), custom_call_target="tpu_custom_call" | custom-call | flops 536870912 | bytes 3145728 | tf_op jit(solution)/shard_map/gathered/pallas_call | solution.py:202
  113.9 0.0 copy-done
  113.9 2.5 %update_first.1 = (bf16[4,128,512]{2,1,0:T(8,128)(2,1)S(1)}, bf16[4,128,512]{2,1,0:T(8,128)(2,1)S(1)}) custom-call(s32[1]{0:T(128)} %bitcast.core_ref.half_ref, s32[2]{0:T(128)S(1)} %bitcast.8, bf16[4,128,1024]{2,1,0:T(8,128)(2,1)S(1)} %all_to_all.10.left_any, bf16[512,1024]{1,0:T(8,128)(2,1)S(1)} %gathered.1.right_ref, bf16[4,2,128,512]{3,2,1,0:T(8,128)(2,1)} %bitcast.10), custom_call_target="tpu_custom_call" | custom-call | flops 536870912 | bytes 3145728 | tf_op jit(solution)/shard_map/update_first/pallas_call | solution.py:269
  116.5 0.0 collective-permute-done.left_ref
  116.5 2.7 %update_second.1 = bf16[4,2,128,512]{3,2,1,0:T(8,128)(2,1)} custom-call(s32[1]{0:T(128)S(6)} %sub.3.half_ref, s32[2]{0:T(128)S(1)} %bitcast.9, bf16[4,128,1024]{2,1,0:T(8,128)(2,1)} %collective-permute-done.left_ref, bf16[512,1024]{1,0:T(8,128)(2,1)S(1)} %gathered.1.right_ref, bf16[4,128,512]{2,1,0:T(8,128)(2,1)S(1)} %get-tuple-element.7.first_ref, ...), custom_call_target="tpu_custom_call" | custom-call | flops 536870912 | bytes 3145728 | tf_op jit(solution)/shard_map/update_second/pallas_call | solution.py:300
Async XLA Ops:
  28.9 15.7 %all-to-all-start = ((bf16[8,16,1024]{2,1,0:T(8,128)(2,1)}), bf16[8,16,1024]{2,1,0:T(8,128)(2,1)S(1)}, u32[]{:S(2)}, u32[]{:S(2)}) async-start(bf16[8,16,1024]{2,1,0:T(8,128)(2,1)} %spread.1), calls=%async_computation | async-start | bytes 524288 | tf_op jit(solution)/shard_map/all_to_all | solution.py:327
  44.6 23.1 %copy-start.1 = (bf16[64,1024]{1,0:T(8,128)(2,1)S(1)}, bf16[64,1024]{1,0:T(8,128)(2,1)}, u32[]{:S(2)}) copy-start(bf16[64,1024]{1,0:T(8,128)(2,1)} %own_hbm.1) | copy-start | bytes 393220
  64.5 52.0 %collective-permute-start = (bf16[4,128,1024]{2,1,0:T(8,128)(2,1)S(1)}, bf16[4,128,1024]{2,1,0:T(8,128)(2,1)}, u32[]{:S(2)}, u32[]{:S(2)}) collective-permute-start(bf16[4,128,1024]{2,1,0:T(8,128)(2,1)S(1)} %all_to_all.10.left_any), channel_id=1, source_target_pairs={{0,1},{1,0},{2,3},{3,2},{4,5},{5,4},{6,7},{7,6},{8,9},{9,8},{10,11... | collective-permute-start | bytes 3145736 | tf_op jit(solution)/shard_map/ppermute | solution.py:316
  67.7 18.6 %collective-permute-start.1 = (bf16[64,1024]{1,0:T(8,128)(2,1)S(1)}, bf16[64,1024]{1,0:T(8,128)(2,1)S(1)}, u32[]{:S(2)}, u32[]{:S(2)}) collective-permute-start(bf16[64,1024]{1,0:T(8,128)(2,1)S(1)} %copy-done.1), channel_id=1, source_target_pairs={{0,512},{128,640},{256,768},{384,896},{512,0},{640,128},{768,256},... | collective-permute-start | bytes 393224 | tf_op jit(solution)/shard_map/ppermute | solution.py:316
  87.3 14.2 %collective-permute-start.3 = (bf16[128,1024]{1,0:T(8,128)(2,1)S(1)}, bf16[128,1024]{1,0:T(8,128)(2,1)S(1)}, u32[]{:S(2)}, u32[]{:S(2)}) collective-permute-start(bf16[128,1024]{1,0:T(8,128)(2,1)S(1)} %join.1), channel_id=1, source_target_pairs={{0,256},{128,384},{256,0},{384,128},{512,768},{640,896},{768,512},... | collective-permute-start | bytes 786440 | tf_op jit(solution)/shard_map/ppermute | solution.py:316
  89.2 15.6 %collective-permute-start.2 = (bf16[128,1024]{1,0:T(8,128)(2,1)S(1)}, bf16[128,1024]{1,0:T(8,128)(2,1)S(1)}, u32[]{:S(2)}, u32[]{:S(2)}) collective-permute-start(bf16[128,1024]{1,0:T(8,128)(2,1)S(1)} %join.1), channel_id=1, source_target_pairs={{0,128},{128,0},{256,384},{384,256},{512,640},{640,512},{768,896},... | collective-permute-start | bytes 786440 | tf_op jit(solution)/shard_map/ppermute | solution.py:316
  102.9 11.1 %copy-start = (s32[2,1]{0,1:T(1,128)S(1)}, s32[2,1]{0,1:T(1,128)}, u32[]{:S(2)}) copy-start(s32[2,1]{0,1:T(1,128)} %param.9) | copy-start | bytes 28
  102.9 9.4 %collective-permute-start.4 = (bf16[128,1024]{1,0:T(8,128)(2,1)}, bf16[128,1024]{1,0:T(8,128)(2,1)S(1)}, u32[]{:S(2)}, u32[]{:S(2)}) collective-permute-start(bf16[128,1024]{1,0:T(8,128)(2,1)} %bitcast.11), channel_id=1, source_target_pairs={{0,128},{128,0},{256,384},{384,256},{512,640},{640,512},{768,896},... | collective-permute-start | bytes 786440 | tf_op jit(solution)/shard_map/ppermute | solution.py:316

commit v3 on v2

--- a/solution.py
+++ b/solution.py
@@ -170,7 +170,7 @@
 
 
 def gathered_kernel(
-    zlo_ref, own_hbm, across_hbm, third_hbm, second_hbm, last_hbm, parts_ref, right_ref, rows_ref, in_sems, out_sems
+    zlo_ref, own_hbm, across_hbm, third_hbm, second_hbm, parts_ref, right_ref, rows_ref, in_sems, out_sems
 ):
     size = own_hbm.shape[0]
     raw = [
@@ -178,10 +178,9 @@
         for at, ref in enumerate((own_hbm, across_hbm, third_hbm))
     ]
     placed = []
-    for pair, ref in ((1, second_hbm), (3, last_hbm)):
-        for at, start in enumerate(block_starts(zlo_ref, PAIRS[pair], size)):
-            place = right_ref.at[pl.ds(start, size)]
-            placed.append(pltpu.make_async_copy(ref.at[pl.ds(at * size, size)], place, out_sems.at[pair // 2, at]))
+    for at, start in enumerate(block_starts(zlo_ref, PAIRS[1], size)):
+        place = right_ref.at[pl.ds(start, size)]
+        placed.append(pltpu.make_async_copy(second_hbm.at[pl.ds(at * size, size)], place, out_sems.at[at]))
     for copy in raw + placed:
         copy.start()
     starts = [start for pair in (0, 2) for start in block_starts(zlo_ref, PAIRS[pair], size)]
@@ -197,22 +196,22 @@
         copy.wait()
 
 
-def gathered(zlo, own, across, third, second, last, parts):
+def gathered(zlo, own, across, third, second, parts):
     size, features = own.shape
     return pl.pallas_call(
         gathered_kernel,
         out_shape=jax.ShapeDtypeStruct((8 * size, features), parts.dtype),
-        in_specs=[SMEM, HBM, ANY, ANY, HBM, ANY, VMEM],
+        in_specs=[SMEM, HBM, ANY, ANY, HBM, VMEM],
         out_specs=VMEM,
         scratch_shapes=[
             pltpu.VMEM((4 * size, features), parts.dtype),
             pltpu.SemaphoreType.DMA((3,)),
-            pltpu.SemaphoreType.DMA((2, 2)),
+            pltpu.SemaphoreType.DMA((2,)),
         ],
         compiler_params=SMALL,
         cost_estimate=factor_cost(4 * size, features, 2 * parts.shape[2], 1),
         name="gathered",
-    )(zlo, in_hbm(own), across, third, in_hbm(second), last, parts)
+    )(zlo, in_hbm(own), across, third, in_hbm(second), parts)
 
 
 def change_tile(tile, tile_rows, active_ref, left_ref, right_ref, trailing_ref, done_ref):
@@ -232,24 +231,31 @@
     return [pl.ds(tile * group, group) for tile in range(tile_rows)]
 
 
-def first_kernel(half_ref, active_ref, left_any, right_ref, trailing_hbm, done_ref, next_ref, left_ref, trailing_ref, sems):
+def first_kernel(
+    half_ref, zlo_ref, active_ref, left_any, right_in, last_any, trailing_hbm, done_ref, next_ref, right_ref,
+    left_ref, trailing_ref, sems,
+):
     half = half_ref[0]
     tile_rows = active_ref.shape[0]
     xs = done_ref.shape[0]
-    spans = tile_spans(xs, tile_rows)
-    steps = []
-    for tile, span in enumerate(spans):
-        steps.append(
-            (
-                pltpu.make_async_copy(left_any.at[span], left_ref.at[span], sems.at[0, tile]),
-                pltpu.make_async_copy(trailing_hbm.at[span, half], trailing_ref.at[span], sems.at[1, tile]),
-            )
+    size = last_any.shape[0] // 2
+    placed = [
+        pltpu.make_async_copy(last_any.at[pl.ds(at * size, size)], right_ref.at[pl.ds(start, size)], sems.at[0, at])
+        for at, start in enumerate(block_starts(zlo_ref, PAIRS[3], size))
+    ]
+    arrivals = [
+        (
+            pltpu.make_async_copy(left_any.at[span], left_ref.at[span], sems.at[3, tile]),
+            pltpu.make_async_copy(trailing_hbm.at[span, half], trailing_ref.at[span], sems.at[1, tile]),
         )
-        for copy in steps[-1]:
-            copy.start()
+        for tile, span in enumerate(tile_spans(xs, tile_rows))
+    ]
     ahead = pltpu.make_async_copy(trailing_hbm.at[pl.ds(0, xs), 1 - half], next_ref, sems.at[2, 0])
-    ahead.start()
-    for tile, pair in enumerate(steps):
+    for copy in placed + [copy for pair in arrivals for copy in pair] + [ahead]:
+        copy.start()
+    for copy in placed:
+        copy.wait()
+    for tile, pair in enumerate(arrivals):
         for copy in pair:
             copy.wait()
         change_tile(tile, tile_rows, active_ref, left_ref, right_ref, trailing_ref, done_ref)
@@ -264,22 +270,23 @@
     )
 
 
-def update_first(half, active, left, right, trailing):
+def update_first(half, zlo, active, left, right, last, trailing):
     shape = left.shape[:2] + trailing.shape[3:]
     return pl.pallas_call(
         first_kernel,
-        out_shape=[jax.ShapeDtypeStruct(shape, trailing.dtype)] * 2,
-        in_specs=[SMEM] * 2 + [ANY, VMEM, HBM],
-        out_specs=[VMEM] * 2,
+        out_shape=[jax.ShapeDtypeStruct(shape, trailing.dtype)] * 2 + [jax.ShapeDtypeStruct(right.shape, right.dtype)],
+        in_specs=[SMEM] * 3 + [ANY, VMEM, ANY, HBM],
+        out_specs=[VMEM] * 3,
         scratch_shapes=[
             pltpu.VMEM(left.shape, left.dtype),
             pltpu.VMEM(shape, trailing.dtype),
-            pltpu.SemaphoreType.DMA((3, active.shape[0])),
+            pltpu.SemaphoreType.DMA((4, 2)),
         ],
+        input_output_aliases={4: 2},
         compiler_params=SMALL,
         cost_estimate=update_cost(left, right),
         name="update_first",
-    )(half, active, left, right, in_hbm(trailing))
+    )(half, zlo, active, left, right, last, in_hbm(trailing))
 
 
 def second_kernel(half_ref, active_ref, left_ref, right_ref, first_ref, trailing_ref, out_hbm, done_ref, sems):
@@ -333,10 +340,10 @@
     second = factor_left(second, parts, 1).reshape(second.shape)
     last = swap(second, "zlo", 1, 8)
     view = trailing.reshape(4, 2, trailing.shape[0] // 8, trailing.shape[1])
-    right = gathered(zlo, panel_right, across, third, second, last, parts)
+    right = gathered(zlo, panel_right, across, third, second, parts)
     other = swap(own, "core", 1, 2)
     flags = active.reshape(-1)
-    first, held = update_first(core, flags, own, right, view)
+    first, held, right = update_first(core, zlo, flags, own, right, last, view)
     result = update_second(1 - core, flags, other, right, first, held, view.shape)
     return result.reshape(trailing.shape)
 

time: 120 us -> 118 us (0.983)
  waiting for transfers between devices: 43.3 us -> 41.7 us
    ppermute x5, waiting for transfers between devices: 32.5 us -> 30.9 us  [swap(): return lax.ppermute(v, axis, [(i, i ^ bit) for i in range(n)])]
where the time goes in v3:
time: 118 us
  blocking collectives  46.3 us (39%)
  waiting for transfers between devices  41.7 us (35%)
  starting transfers between devices  16.4 us (14%)
  Pallas kernels  13.4 us (11%)
    ppermute x5, waiting for transfers between devices, swap(): return lax.ppermute(v, axis, [(i, i ^ bit) for i in range(n)])  30.9 us
    all_gather x1, blocking collectives, local(): near = lax.all_gather(panel_left, ('zhi', 'core'), axis=0, tiled=True)  28.1 us
    all_to_all x1, blocking collectives, local(): own = lax.all_to_all(wide, 'x', 0, 0)  18.2 us
    ppermute x5, starting transfers between devices, swap(): return lax.ppermute(v, axis, [(i, i ^ bit) for i in range(n)])  13 us
    all_to_all x1, waiting for transfers between devices, local(): line = lax.all_to_all(spread, 'y', 0, 0).reshape(-1, features)  10.8 us
    all_to_all x1, starting transfers between devices, local(): line = lax.all_to_all(spread, 'y', 0, 0).reshape(-1, features)  3.42 us
    pallas_call x2, Pallas kernels, factor_left(): pl.pallas_call(factor_left_kernel, out_shape=pltpu.HBM((peers,) + rows.sh...  2.99 us
    pallas_call x1, Pallas kernels, update_first(): pl.pallas_call(first_kernel, out_shape=[jax.ShapeDtypeStruct(shape, trail...  2.89 us
  transfers between devices with their start and end apart: 6, of which 4 were waited for; matrix products, arithmetic and copies ran while one was open for 0% of the time, Pallas kernels for 7%

profile of v3, /device:TPU:1, one launch (start us, length us, event | category | flops | bytes accessed | tf_op | source)
XLA Modules:
  0.0 117.9 jit_solution(900060030544423110)
XLA Ops:
  0.0 28.1 %all_gather.3.near_ref = bf16[32,1024]{1,0:T(8,128)(2,1)S(1)} all-gather(bf16[8,1024]{1,0:T(8,128)(2,1)} %param.6), channel_id=1, replica_groups=mesh['zlo'=8,'x'=4,'zhi'=2,'y'=8,'core'=2] {'zhi','core'}, dimensions={0}, use_global_device_ids=true | all-gather | bytes 81920 | tf_op jit(solution)/shard_map/all_gather | solution.py:331
  28.1 0.8 spread.1
  28.9 3.4 %all-to-all-start = ((bf16[8,16,1024]{2,1,0:T(8,128)(2,1)}), bf16[8,16,1024]{2,1,0:T(8,128)(2,1)S(1)}, u32[]{:S(2)}, u32[]{:S(2)}) async-start(bf16[8,16,1024]{2,1,0:T(8,128)(2,1)} %spread.1), calls=%async_computation | async-start | bytes 524288 | tf_op jit(solution)/shard_map/all_to_all | solution.py:334
  32.3 1.5 %split.1.parts_ref = bf16[2,2,256,768]{3,2,1,0:T(8,128)(2,1)S(1)} custom-call(f32[2,512,512]{2,1,0:T(8,128)} %inverse_hbm.1), custom_call_target="tpu_custom_call" | custom-call | flops 2097152 | bytes 4194304 | tf_op jit(solution)/shard_map/split/pallas_call | solution.py:100
  33.8 10.8 %all-to-all-done = bf16[8,16,1024]{2,1,0:T(8,128)(2,1)S(1)} async-done(((bf16[8,16,1024]{2,1,0:T(8,128)(2,1)}), bf16[8,16,1024]{2,1,0:T(8,128)(2,1)S(1)}, u32[]{:S(2)}, u32[]{:S(2)}) %all-to-all-start) | async-done | bytes 262176 | tf_op jit(solution)/shard_map/all_to_all | solution.py:334
  44.6 0.0 copy-start.1
  44.6 1.6 %factor_left.1 = bf16[4,128,1024]{2,1,0:T(8,128)(2,1)} custom-call(bf16[128,1024]{1,0:T(8,128)(2,1)S(1)} %bitcast.7, bf16[2,2,256,768]{3,2,1,0:T(8,128)(2,1)S(1)} %split.1.parts_ref), custom_call_target="tpu_custom_call" | custom-call | flops 268435456 | bytes 3407872 | tf_op jit(solution)/shard_map/factor_left/pallas_call | solution.py:153
  46.2 18.2 %all_to_all.10.left_any = bf16[4,128,1024]{2,1,0:T(8,128)(2,1)S(1)} all-to-all(bf16[4,128,1024]{2,1,0:T(8,128)(2,1)} %factor_left.1), channel_id=1, replica_groups=mesh['zlo'=8,'x'=4,'zhi'=2,'y'=8,'core'=2] {'x'}, dimensions={0} | all-to-all | bytes 2097152 | tf_op jit(solution)/shard_map/all_to_all | solution.py:339
  64.5 3.2 %collective-permute-start = (bf16[4,128,1024]{2,1,0:T(8,128)(2,1)S(1)}, bf16[4,128,1024]{2,1,0:T(8,128)(2,1)}, u32[]{:S(2)}, u32[]{:S(2)}) collective-permute-start(bf16[4,128,1024]{2,1,0:T(8,128)(2,1)S(1)} %all_to_all.10.left_any), channel_id=1, source_target_pairs={{0,1},{1,0},{2,3},{3,2},{4,5},{5,4},{6,7},{7,6},{8,9},{9,8},{10,11... | collective-permute-start | bytes 3145736 | tf_op jit(solution)/shard_map/ppermute | solution.py:323
  67.7 0.0 copy-done.1
  67.7 3.9 %collective-permute-start.1 = (bf16[64,1024]{1,0:T(8,128)(2,1)S(1)}, bf16[64,1024]{1,0:T(8,128)(2,1)S(1)}, u32[]{:S(2)}, u32[]{:S(2)}) collective-permute-start(bf16[64,1024]{1,0:T(8,128)(2,1)S(1)} %copy-done.1), channel_id=1, source_target_pairs={{0,512},{128,640},{256,768},{384,896},{512,0},{640,128},{768,256},... | collective-permute-start | bytes 393224 | tf_op jit(solution)/shard_map/ppermute | solution.py:323
  71.6 14.8 %collective-permute-done.1.second_any.across_hbm = bf16[64,1024]{1,0:T(8,128)(2,1)S(1)} collective-permute-done((bf16[64,1024]{1,0:T(8,128)(2,1)S(1)}, bf16[64,1024]{1,0:T(8,128)(2,1)S(1)}, u32[]{:S(2)}, u32[]{:S(2)}) %collective-permute-start.1) | collective-permute-done | bytes 131104 | tf_op jit(solution)/shard_map/ppermute | solution.py:323
  86.3 0.9 join.1
  87.3 1.9 %collective-permute-start.3 = (bf16[128,1024]{1,0:T(8,128)(2,1)S(1)}, bf16[128,1024]{1,0:T(8,128)(2,1)S(1)}, u32[]{:S(2)}, u32[]{:S(2)}) collective-permute-start(bf16[128,1024]{1,0:T(8,128)(2,1)S(1)} %join.1), channel_id=1, source_target_pairs={{0,256},{128,384},{256,0},{384,128},{512,768},{640,896},{768,512},... | collective-permute-start | bytes 786440 | tf_op jit(solution)/shard_map/ppermute | solution.py:323
  89.2 2.1 %collective-permute-start.2 = (bf16[128,1024]{1,0:T(8,128)(2,1)S(1)}, bf16[128,1024]{1,0:T(8,128)(2,1)S(1)}, u32[]{:S(2)}, u32[]{:S(2)}) collective-permute-start(bf16[128,1024]{1,0:T(8,128)(2,1)S(1)} %join.1), channel_id=1, source_target_pairs={{0,128},{128,0},{256,384},{384,256},{512,640},{640,512},{768,896},... | collective-permute-start | bytes 786440 | tf_op jit(solution)/shard_map/ppermute | solution.py:323
  91.3 10.2 %collective-permute-done.3.rows_ref = bf16[128,1024]{1,0:T(8,128)(2,1)S(1)} collective-permute-done((bf16[128,1024]{1,0:T(8,128)(2,1)S(1)}, bf16[128,1024]{1,0:T(8,128)(2,1)S(1)}, u32[]{:S(2)}, u32[]{:S(2)}) %collective-permute-start.3) | collective-permute-done | bytes 262176 | tf_op jit(solution)/shard_map/ppermute | solution.py:323
  101.5 1.4 %factor_right.1 = bf16[1,128,1024]{2,1,0:T(8,128)(2,1)} custom-call(bf16[128,1024]{1,0:T(8,128)(2,1)S(1)} %collective-permute-done.3.rows_ref, bf16[2,2,256,768]{3,2,1,0:T(8,128)(2,1)S(1)} %split.1.parts_ref), custom_call_target="tpu_custom_call" | custom-call | flops 268435456 | bytes 2621440 | tf_op jit(solution)/shard_map/factor_right/pallas_call | solution.py:153
  102.9 0.0 copy-start
  102.9 1.9 %collective-permute-start.4 = (bf16[128,1024]{1,0:T(8,128)(2,1)}, bf16[128,1024]{1,0:T(8,128)(2,1)S(1)}, u32[]{:S(2)}, u32[]{:S(2)}) collective-permute-start(bf16[128,1024]{1,0:T(8,128)(2,1)} %bitcast.11), channel_id=1, source_target_pairs={{0,128},{128,0},{256,384},{384,256},{512,640},{640,512},{768,896},... | collective-permute-start | bytes 786440 | tf_op jit(solution)/shard_map/ppermute | solution.py:323
  104.8 0.0 collective-permute-done.2.third_hbm
  104.8 1.6 %gathered.1.right_in = bf16[512,1024]{1,0:T(8,128)(2,1)S(1)} custom-call(s32[1]{0:T(128)} %bitcast.3.zlo_ref, bf16[64,1024]{1,0:T(8,128)(2,1)} %own_hbm.1, bf16[64,1024]{1,0:T(8,128)(2,1)S(1)} %collective-permute-done.1.second_any.across_hbm, bf16[128,1024]{1,0:T(8,128)(2,1)S(1)} %collective-permute-done.2.third_hbm, bf16[128,1024]{1,0:T(8,128)(2,1)} %bitcast.12, ...), custom_call_target="tpu_custom_call" | custom-call | flops 536870912 | bytes 3145728 | tf_op jit(solution)/shard_map/gathered/pallas_call | solution.py:201
  106.4 5.9 %collective-permute-done.4.last_any = bf16[128,1024]{1,0:T(8,128)(2,1)S(1)} collective-permute-done((bf16[128,1024]{1,0:T(8,128)(2,1)}, bf16[128,1024]{1,0:T(8,128)(2,1)S(1)}, u32[]{:S(2)}, u32[]{:S(2)}) %collective-permute-start.4) | collective-permute-done | bytes 262176 | tf_op jit(solution)/shard_map/ppermute | solution.py:323
  112.3 0.0 copy-done
  112.3 2.9 %update_first.1 = (bf16[4,128,512]{2,1,0:T(8,128)(2,1)S(1)}, bf16[4,128,512]{2,1,0:T(8,128)(2,1)S(1)}, bf16[512,1024]{1,0:T(8,128)(2,1)S(1)}) custom-call(s32[1]{0:T(128)} %bitcast.core_ref.half_ref, s32[1]{0:T(128)} %bitcast.3.zlo_ref, s32[2]{0:T(128)S(1)} %bitcast.8, ...), custom_call_target="tpu_custom_call", output_to_operand_aliasing={{2}: (4, {})} | custom-call | flops 536870912 | bytes 3145728 | tf_op jit(solution)/shard_map/update_first/pallas_call | solution.py:275
  115.2 0.0 collective-permute-done.left_ref
  115.2 2.7 %update_second.1 = bf16[4,2,128,512]{3,2,1,0:T(8,128)(2,1)} custom-call(s32[1]{0:T(128)S(6)} %sub.3.half_ref, s32[2]{0:T(128)S(1)} %bitcast.9, bf16[4,128,1024]{2,1,0:T(8,128)(2,1)} %collective-permute-done.left_ref, bf16[512,1024]{1,0:T(8,128)(2,1)S(1)} %get-tuple-element.8.right_ref, bf16[4,128,512]{2,1,0:T(8,128)(2,1)S(1)} %get-tuple-element.9.first_ref, ...), custom_call_target="tpu_custom_call" | custom-call | flops 536870912 | bytes 3145728 | tf_op jit(solution)/shard_map/update_second/pallas_call | solution.py:307
Async XLA Ops:
  28.9 15.7 %all-to-all-start = ((bf16[8,16,1024]{2,1,0:T(8,128)(2,1)}), bf16[8,16,1024]{2,1,0:T(8,128)(2,1)S(1)}, u32[]{:S(2)}, u32[]{:S(2)}) async-start(bf16[8,16,1024]{2,1,0:T(8,128)(2,1)} %spread.1), calls=%async_computation | async-start | bytes 524288 | tf_op jit(solution)/shard_map/all_to_all | solution.py:334
  44.6 23.1 %copy-start.1 = (bf16[64,1024]{1,0:T(8,128)(2,1)S(1)}, bf16[64,1024]{1,0:T(8,128)(2,1)}, u32[]{:S(2)}) copy-start(bf16[64,1024]{1,0:T(8,128)(2,1)} %own_hbm.1) | copy-start | bytes 393220
  64.5 50.7 %collective-permute-start = (bf16[4,128,1024]{2,1,0:T(8,128)(2,1)S(1)}, bf16[4,128,1024]{2,1,0:T(8,128)(2,1)}, u32[]{:S(2)}, u32[]{:S(2)}) collective-permute-start(bf16[4,128,1024]{2,1,0:T(8,128)(2,1)S(1)} %all_to_all.10.left_any), channel_id=1, source_target_pairs={{0,1},{1,0},{2,3},{3,2},{4,5},{5,4},{6,7},{7,6},{8,9},{9,8},{10,11... | collective-permute-start | bytes 3145736 | tf_op jit(solution)/shard_map/ppermute | solution.py:323
  67.7 18.6 %collective-permute-start.1 = (bf16[64,1024]{1,0:T(8,128)(2,1)S(1)}, bf16[64,1024]{1,0:T(8,128)(2,1)S(1)}, u32[]{:S(2)}, u32[]{:S(2)}) collective-permute-start(bf16[64,1024]{1,0:T(8,128)(2,1)S(1)} %copy-done.1), channel_id=1, source_target_pairs={{0,512},{128,640},{256,768},{384,896},{512,0},{640,128},{768,256},... | collective-permute-start | bytes 393224 | tf_op jit(solution)/shard_map/ppermute | solution.py:323
  87.3 14.2 %collective-permute-start.3 = (bf16[128,1024]{1,0:T(8,128)(2,1)S(1)}, bf16[128,1024]{1,0:T(8,128)(2,1)S(1)}, u32[]{:S(2)}, u32[]{:S(2)}) collective-permute-start(bf16[128,1024]{1,0:T(8,128)(2,1)S(1)} %join.1), channel_id=1, source_target_pairs={{0,256},{128,384},{256,0},{384,128},{512,768},{640,896},{768,512},... | collective-permute-start | bytes 786440 | tf_op jit(solution)/shard_map/ppermute | solution.py:323
  89.2 15.6 %collective-permute-start.2 = (bf16[128,1024]{1,0:T(8,128)(2,1)S(1)}, bf16[128,1024]{1,0:T(8,128)(2,1)S(1)}, u32[]{:S(2)}, u32[]{:S(2)}) collective-permute-start(bf16[128,1024]{1,0:T(8,128)(2,1)S(1)} %join.1), channel_id=1, source_target_pairs={{0,128},{128,0},{256,384},{384,256},{512,640},{640,512},{768,896},... | collective-permute-start | bytes 786440 | tf_op jit(solution)/shard_map/ppermute | solution.py:323
  102.9 9.4 %copy-start = (s32[2,1]{0,1:T(1,128)S(1)}, s32[2,1]{0,1:T(1,128)}, u32[]{:S(2)}) copy-start(s32[2,1]{0,1:T(1,128)} %param.9) | copy-start | bytes 28
  102.9 9.4 %collective-permute-start.4 = (bf16[128,1024]{1,0:T(8,128)(2,1)}, bf16[128,1024]{1,0:T(8,128)(2,1)S(1)}, u32[]{:S(2)}, u32[]{:S(2)}) collective-permute-start(bf16[128,1024]{1,0:T(8,128)(2,1)} %bitcast.11), channel_id=1, source_target_pairs={{0,128},{128,0},{256,384},{384,256},{512,640},{640,512},{768,896},... | collective-permute-start | bytes 786440 | tf_op jit(solution)/shard_map/ppermute | solution.py:323

commit v4 on v3

--- a/solution.py
+++ b/solution.py
@@ -170,7 +170,8 @@
 
 
 def gathered_kernel(
-    zlo_ref, own_hbm, across_hbm, third_hbm, second_hbm, parts_ref, right_ref, rows_ref, in_sems, out_sems
+    zlo_ref, half_ref, own_hbm, across_hbm, third_hbm, second_hbm, parts_ref, trailing_hbm, right_ref, held_ref,
+    rows_ref, in_sems, out_sems, held_sem,
 ):
     size = own_hbm.shape[0]
     raw = [
@@ -181,6 +182,8 @@
     for at, start in enumerate(block_starts(zlo_ref, PAIRS[1], size)):
         place = right_ref.at[pl.ds(start, size)]
         placed.append(pltpu.make_async_copy(second_hbm.at[pl.ds(at * size, size)], place, out_sems.at[at]))
+    xs = held_ref.shape[0]
+    placed.append(pltpu.make_async_copy(trailing_hbm.at[pl.ds(0, xs), half_ref[0]], held_ref, held_sem))
     for copy in raw + placed:
         copy.start()
     starts = [start for pair in (0, 2) for start in block_starts(zlo_ref, PAIRS[pair], size)]
@@ -196,22 +199,27 @@
         copy.wait()
 
 
-def gathered(zlo, own, across, third, second, parts):
+def gathered(zlo, half, own, across, third, second, parts, trailing):
     size, features = own.shape
+    xs, _, rows, cols = trailing.shape
     return pl.pallas_call(
         gathered_kernel,
-        out_shape=jax.ShapeDtypeStruct((8 * size, features), parts.dtype),
-        in_specs=[SMEM, HBM, ANY, ANY, HBM, VMEM],
-        out_specs=VMEM,
+        out_shape=[
+            jax.ShapeDtypeStruct((8 * size, features), parts.dtype),
+            jax.ShapeDtypeStruct((xs, rows, cols), trailing.dtype),
+        ],
+        in_specs=[SMEM, SMEM, HBM, ANY, ANY, HBM, VMEM, HBM],
+        out_specs=[VMEM] * 2,
         scratch_shapes=[
             pltpu.VMEM((4 * size, features), parts.dtype),
             pltpu.SemaphoreType.DMA((3,)),
             pltpu.SemaphoreType.DMA((2,)),
+            pltpu.SemaphoreType.DMA,
         ],
         compiler_params=SMALL,
         cost_estimate=factor_cost(4 * size, features, 2 * parts.shape[2], 1),
         name="gathered",
-    )(zlo, in_hbm(own), across, third, in_hbm(second), parts)
+    )(zlo, half, in_hbm(own), across, third, in_hbm(second), parts, in_hbm(trailing))
 
 
 def change_tile(tile, tile_rows, active_ref, left_ref, right_ref, trailing_ref, done_ref):
@@ -232,32 +240,26 @@
 
 
 def first_kernel(
-    half_ref, zlo_ref, active_ref, left_any, right_in, last_any, trailing_hbm, done_ref, next_ref, right_ref,
-    left_ref, trailing_ref, sems,
+    half_ref, zlo_ref, active_ref, left_any, right_in, last_any, trailing_ref, trailing_hbm, done_ref, next_ref, right_ref,
+    left_ref, sems,
 ):
-    half = half_ref[0]
     tile_rows = active_ref.shape[0]
-    xs = done_ref.shape[0]
     size = last_any.shape[0] // 2
     placed = [
         pltpu.make_async_copy(last_any.at[pl.ds(at * size, size)], right_ref.at[pl.ds(start, size)], sems.at[0, at])
         for at, start in enumerate(block_starts(zlo_ref, PAIRS[3], size))
     ]
     arrivals = [
-        (
-            pltpu.make_async_copy(left_any.at[span], left_ref.at[span], sems.at[3, tile]),
-            pltpu.make_async_copy(trailing_hbm.at[span, half], trailing_ref.at[span], sems.at[1, tile]),
-        )
-        for tile, span in enumerate(tile_spans(xs, tile_rows))
+        pltpu.make_async_copy(left_any.at[span], left_ref.at[span], sems.at[1, tile])
+        for tile, span in enumerate(tile_spans(done_ref.shape[0], tile_rows))
     ]
-    ahead = pltpu.make_async_copy(trailing_hbm.at[pl.ds(0, xs), 1 - half], next_ref, sems.at[2, 0])
-    for copy in placed + [copy for pair in arrivals for copy in pair] + [ahead]:
+    ahead = pltpu.make_async_copy(trailing_hbm.at[pl.ds(0, done_ref.shape[0]), 1 - half_ref[0]], next_ref, sems.at[2, 0])
+    for copy in placed + arrivals + [ahead]:
         copy.start()
     for copy in placed:
         copy.wait()
-    for tile, pair in enumerate(arrivals):
-        for copy in pair:
-            copy.wait()
+    for tile, copy in enumerate(arrivals):
+        copy.wait()
         change_tile(tile, tile_rows, active_ref, left_ref, right_ref, trailing_ref, done_ref)
     ahead.wait()
 
@@ -270,23 +272,19 @@
     )
 
 
-def update_first(half, zlo, active, left, right, last, trailing):
-    shape = left.shape[:2] + trailing.shape[3:]
+def update_first(half, zlo, active, left, right, last, held, trailing):
     return pl.pallas_call(
         first_kernel,
-        out_shape=[jax.ShapeDtypeStruct(shape, trailing.dtype)] * 2 + [jax.ShapeDtypeStruct(right.shape, right.dtype)],
-        in_specs=[SMEM] * 3 + [ANY, VMEM, ANY, HBM],
+        out_shape=[jax.ShapeDtypeStruct(held.shape, held.dtype)] * 2
+        + [jax.ShapeDtypeStruct(right.shape, right.dtype)],
+        in_specs=[SMEM] * 3 + [ANY, VMEM, ANY, VMEM, HBM],
         out_specs=[VMEM] * 3,
-        scratch_shapes=[
-            pltpu.VMEM(left.shape, left.dtype),
-            pltpu.VMEM(shape, trailing.dtype),
-            pltpu.SemaphoreType.DMA((4, 2)),
-        ],
+        scratch_shapes=[pltpu.VMEM(left.shape, left.dtype), pltpu.SemaphoreType.DMA((3, 2))],
         input_output_aliases={4: 2},
         compiler_params=SMALL,
         cost_estimate=update_cost(left, right),
         name="update_first",
-    )(half, zlo, active, left, right, last, in_hbm(trailing))
+    )(half, zlo, active, left, right, last, held, in_hbm(trailing))
 
 
 def second_kernel(half_ref, active_ref, left_ref, right_ref, first_ref, trailing_ref, out_hbm, done_ref, sems):
@@ -340,11 +338,11 @@
     second = factor_left(second, parts, 1).reshape(second.shape)
     last = swap(second, "zlo", 1, 8)
     view = trailing.reshape(4, 2, trailing.shape[0] // 8, trailing.shape[1])
-    right = gathered(zlo, panel_right, across, third, second, parts)
+    right, held = gathered(zlo, core, panel_right, across, third, second, parts, view)
     other = swap(own, "core", 1, 2)
     flags = active.reshape(-1)
-    first, held, right = update_first(core, zlo, flags, own, right, last, view)
-    result = update_second(1 - core, flags, other, right, first, held, view.shape)
+    first, ahead, right = update_first(core, zlo, flags, own, right, last, held, view)
+    result = update_second(1 - core, flags, other, right, first, ahead, view.shape)
     return result.reshape(trailing.shape)
 
 

time: 118 us -> 118 us (level)
  transfers between devices with their start and end apart: 6 -> 6, of which waited for: 4 -> 4; matrix products, arithmetic and copies ran while one was open for 0% -> 0% of each run, Pallas kernels for 7% -> 6%
where the time goes in v4:
time: 118 us; the launch traced here: 117 us
  blocking collectives  46.3 us (39%)
  waiting for transfers between devices  41.6 us (35%)
  starting transfers between devices  16.4 us (14%)
  Pallas kernels  12.5 us (11%)
    ppermute x5, waiting for transfers between devices, swap(): return lax.ppermute(v, axis, [(i, i ^ bit) for i in range(n)])  30.9 us
    all_gather x1, blocking collectives, local(): near = lax.all_gather(panel_left, ('zhi', 'core'), axis=0, tiled=True)  28.1 us
    all_to_all x1, blocking collectives, local(): own = lax.all_to_all(wide, 'x', 0, 0)  18.2 us
    ppermute x5, starting transfers between devices, swap(): return lax.ppermute(v, axis, [(i, i ^ bit) for i in range(n)])  13 us
    all_to_all x1, waiting for transfers between devices, local(): line = lax.all_to_all(spread, 'y', 0, 0).reshape(-1, features)  10.8 us
    all_to_all x1, starting transfers between devices, local(): line = lax.all_to_all(spread, 'y', 0, 0).reshape(-1, features)  3.42 us
    pallas_call x2, Pallas kernels, factor_left(): pl.pallas_call(factor_left_kernel, out_shape=pltpu.HBM((peers,) + rows.sh...  2.99 us
    pallas_call x1, Pallas kernels, update_second(): pl.pallas_call(second_kernel, out_shape=pltpu.HBM(shape, first.dtype), in...  2.72 us
  transfers between devices with their start and end apart: 6, of which 4 were waited for; matrix products, arithmetic and copies ran while one was open for 0% of the time, Pallas kernels for 6%

profile of v4, /device:TPU:1, one launch (start us, length us, event | category | flops | bytes accessed | tf_op | source)
XLA Modules:
  0.0 117.1 jit_solution(12940297830794582478)
XLA Ops:
  0.0 28.1 %all_gather.3.near_ref = bf16[32,1024]{1,0:T(8,128)(2,1)S(1)} all-gather(bf16[8,1024]{1,0:T(8,128)(2,1)} %param.6), channel_id=1, replica_groups=mesh['zlo'=8,'x'=4,'zhi'=2,'y'=8,'core'=2] {'zhi','core'}, dimensions={0}, use_global_device_ids=true | all-gather | bytes 81920 | tf_op jit(solution)/shard_map/all_gather | solution.py:329
  28.1 0.8 spread.1
  28.9 3.4 %all-to-all-start = ((bf16[8,16,1024]{2,1,0:T(8,128)(2,1)}), bf16[8,16,1024]{2,1,0:T(8,128)(2,1)S(1)}, u32[]{:S(2)}, u32[]{:S(2)}) async-start(bf16[8,16,1024]{2,1,0:T(8,128)(2,1)} %spread.1), calls=%async_computation | async-start | bytes 524288 | tf_op jit(solution)/shard_map/all_to_all | solution.py:332
  32.3 1.5 %split.1.parts_ref = bf16[2,2,256,768]{3,2,1,0:T(8,128)(2,1)S(1)} custom-call(f32[2,512,512]{2,1,0:T(8,128)} %inverse_hbm.1), custom_call_target="tpu_custom_call" | custom-call | flops 2097152 | bytes 4194304 | tf_op jit(solution)/shard_map/split/pallas_call | solution.py:100
  33.8 10.8 %all-to-all-done = bf16[8,16,1024]{2,1,0:T(8,128)(2,1)S(1)} async-done(((bf16[8,16,1024]{2,1,0:T(8,128)(2,1)}), bf16[8,16,1024]{2,1,0:T(8,128)(2,1)S(1)}, u32[]{:S(2)}, u32[]{:S(2)}) %all-to-all-start) | async-done | bytes 262176 | tf_op jit(solution)/shard_map/all_to_all | solution.py:332
  44.6 0.0 copy-start.1
  44.6 1.6 %factor_left.1 = bf16[4,128,1024]{2,1,0:T(8,128)(2,1)} custom-call(bf16[128,1024]{1,0:T(8,128)(2,1)S(1)} %bitcast.7, bf16[2,2,256,768]{3,2,1,0:T(8,128)(2,1)S(1)} %split.1.parts_ref), custom_call_target="tpu_custom_call" | custom-call | flops 268435456 | bytes 3407872 | tf_op jit(solution)/shard_map/factor_left/pallas_call | solution.py:153
  46.2 18.2 %all_to_all.10.left_any = bf16[4,128,1024]{2,1,0:T(8,128)(2,1)S(1)} all-to-all(bf16[4,128,1024]{2,1,0:T(8,128)(2,1)} %factor_left.1), channel_id=1, replica_groups=mesh['zlo'=8,'x'=4,'zhi'=2,'y'=8,'core'=2] {'x'}, dimensions={0} | all-to-all | bytes 2097152 | tf_op jit(solution)/shard_map/all_to_all | solution.py:337
  64.5 3.2 %collective-permute-start = (bf16[4,128,1024]{2,1,0:T(8,128)(2,1)S(1)}, bf16[4,128,1024]{2,1,0:T(8,128)(2,1)}, u32[]{:S(2)}, u32[]{:S(2)}) collective-permute-start(bf16[4,128,1024]{2,1,0:T(8,128)(2,1)S(1)} %all_to_all.10.left_any), channel_id=1, source_target_pairs={{0,1},{1,0},{2,3},{3,2},{4,5},{5,4},{6,7},{7,6},{8,9},{9,8},{10,11... | collective-permute-start | bytes 3145736 | tf_op jit(solution)/shard_map/ppermute | solution.py:321
  67.7 0.0 copy-done.1
  67.7 3.9 %collective-permute-start.1 = (bf16[64,1024]{1,0:T(8,128)(2,1)S(1)}, bf16[64,1024]{1,0:T(8,128)(2,1)S(1)}, u32[]{:S(2)}, u32[]{:S(2)}) collective-permute-start(bf16[64,1024]{1,0:T(8,128)(2,1)S(1)} %copy-done.1), channel_id=1, source_target_pairs={{0,512},{128,640},{256,768},{384,896},{512,0},{640,128},{768,256},... | collective-permute-start | bytes 393224 | tf_op jit(solution)/shard_map/ppermute | solution.py:321
  71.6 14.8 %collective-permute-done.1.second_any.across_hbm = bf16[64,1024]{1,0:T(8,128)(2,1)S(1)} collective-permute-done((bf16[64,1024]{1,0:T(8,128)(2,1)S(1)}, bf16[64,1024]{1,0:T(8,128)(2,1)S(1)}, u32[]{:S(2)}, u32[]{:S(2)}) %collective-permute-start.1) | collective-permute-done | bytes 131104 | tf_op jit(solution)/shard_map/ppermute | solution.py:321
  86.3 0.9 join.1
  87.3 1.9 %collective-permute-start.3 = (bf16[128,1024]{1,0:T(8,128)(2,1)S(1)}, bf16[128,1024]{1,0:T(8,128)(2,1)S(1)}, u32[]{:S(2)}, u32[]{:S(2)}) collective-permute-start(bf16[128,1024]{1,0:T(8,128)(2,1)S(1)} %join.1), channel_id=1, source_target_pairs={{0,256},{128,384},{256,0},{384,128},{512,768},{640,896},{768,512},... | collective-permute-start | bytes 786440 | tf_op jit(solution)/shard_map/ppermute | solution.py:321
  89.2 2.1 %collective-permute-start.2 = (bf16[128,1024]{1,0:T(8,128)(2,1)S(1)}, bf16[128,1024]{1,0:T(8,128)(2,1)S(1)}, u32[]{:S(2)}, u32[]{:S(2)}) collective-permute-start(bf16[128,1024]{1,0:T(8,128)(2,1)S(1)} %join.1), channel_id=1, source_target_pairs={{0,128},{128,0},{256,384},{384,256},{512,640},{640,512},{768,896},... | collective-permute-start | bytes 786440 | tf_op jit(solution)/shard_map/ppermute | solution.py:321
  91.3 10.2 %collective-permute-done.3.rows_ref = bf16[128,1024]{1,0:T(8,128)(2,1)S(1)} collective-permute-done((bf16[128,1024]{1,0:T(8,128)(2,1)S(1)}, bf16[128,1024]{1,0:T(8,128)(2,1)S(1)}, u32[]{:S(2)}, u32[]{:S(2)}) %collective-permute-start.3) | collective-permute-done | bytes 262176 | tf_op jit(solution)/shard_map/ppermute | solution.py:321
  101.5 1.4 %factor_right.1 = bf16[1,128,1024]{2,1,0:T(8,128)(2,1)} custom-call(bf16[128,1024]{1,0:T(8,128)(2,1)S(1)} %collective-permute-done.3.rows_ref, bf16[2,2,256,768]{3,2,1,0:T(8,128)(2,1)S(1)} %split.1.parts_ref), custom_call_target="tpu_custom_call" | custom-call | flops 268435456 | bytes 2621440 | tf_op jit(solution)/shard_map/factor_right/pallas_call | solution.py:153
  102.9 0.0 copy-start
  102.9 1.9 %collective-permute-start.4 = (bf16[128,1024]{1,0:T(8,128)(2,1)}, bf16[128,1024]{1,0:T(8,128)(2,1)S(1)}, u32[]{:S(2)}, u32[]{:S(2)}) collective-permute-start(bf16[128,1024]{1,0:T(8,128)(2,1)} %bitcast.12), channel_id=1, source_target_pairs={{0,128},{128,0},{256,384},{384,256},{512,640},{640,512},{768,896},... | collective-permute-start | bytes 786440 | tf_op jit(solution)/shard_map/ppermute | solution.py:321
  104.8 0.0 collective-permute-done.2.third_hbm
  104.8 1.6 %gathered.1 = (bf16[512,1024]{1,0:T(8,128)(2,1)S(1)}, bf16[4,128,512]{2,1,0:T(8,128)(2,1)S(1)}) custom-call(s32[1]{0:T(128)} %bitcast.3.zlo_ref, s32[1]{0:T(128)} %bitcast.core_ref.half_ref, bf16[64,1024]{1,0:T(8,128)(2,1)} %own_hbm.1, bf16[64,1024]{1,0:T(8,128)(2,1)S(1)} %collective-permute-done.1.second_any.across_hbm, ...), custom_call_target="tpu_custom_call" | custom-call | flops 536870912 | bytes 3145728 | tf_op jit(solution)/shard_map/gathered/pallas_call | solution.py:205
  106.4 5.9 %collective-permute-done.4.last_any = bf16[128,1024]{1,0:T(8,128)(2,1)S(1)} collective-permute-done((bf16[128,1024]{1,0:T(8,128)(2,1)}, bf16[128,1024]{1,0:T(8,128)(2,1)S(1)}, u32[]{:S(2)}, u32[]{:S(2)}) %collective-permute-start.4) | collective-permute-done | bytes 262176 | tf_op jit(solution)/shard_map/ppermute | solution.py:321
  112.3 0.0 copy-done
  112.3 2.0 %update_first.1 = (bf16[4,128,512]{2,1,0:T(8,128)(2,1)S(1)}, bf16[4,128,512]{2,1,0:T(8,128)(2,1)S(1)}, bf16[512,1024]{1,0:T(8,128)(2,1)S(1)}) custom-call(s32[1]{0:T(128)} %bitcast.core_ref.half_ref, s32[1]{0:T(128)} %bitcast.3.zlo_ref, s32[2]{0:T(128)S(1)} %bitcast.8, ...), custom_call_target="tpu_custom_call", output_to_operand_aliasing={{2}: (4, {})} | custom-call | flops 536870912 | bytes 3145728 | tf_op jit(solution)/shard_map/update_first/pallas_call | solution.py:276
  114.4 0.0 collective-permute-done.left_ref
  114.4 2.7 %update_second.1 = bf16[4,2,128,512]{3,2,1,0:T(8,128)(2,1)} custom-call(s32[1]{0:T(128)S(6)} %sub.3.half_ref, s32[2]{0:T(128)S(1)} %bitcast.9, bf16[4,128,1024]{2,1,0:T(8,128)(2,1)} %collective-permute-done.left_ref, bf16[512,1024]{1,0:T(8,128)(2,1)S(1)} %get-tuple-element.12.right_ref, bf16[4,128,512]{2,1,0:T(8,128)(2,1)S(1)} %get-tuple-element.13.first_ref, ...), custom_call_target="tpu_custom_call" | custom-call | flops 536870912 | bytes 3145728 | tf_op jit(solution)/shard_map/update_second/pallas_call | solution.py:305
Async XLA Ops:
  28.9 15.7 %all-to-all-start = ((bf16[8,16,1024]{2,1,0:T(8,128)(2,1)}), bf16[8,16,1024]{2,1,0:T(8,128)(2,1)S(1)}, u32[]{:S(2)}, u32[]{:S(2)}) async-start(bf16[8,16,1024]{2,1,0:T(8,128)(2,1)} %spread.1), calls=%async_computation | async-start | bytes 524288 | tf_op jit(solution)/shard_map/all_to_all | solution.py:332
  44.6 23.1 %copy-start.1 = (bf16[64,1024]{1,0:T(8,128)(2,1)S(1)}, bf16[64,1024]{1,0:T(8,128)(2,1)}, u32[]{:S(2)}) copy-start(bf16[64,1024]{1,0:T(8,128)(2,1)} %own_hbm.1) | copy-start | bytes 393220
  64.5 49.9 %collective-permute-start = (bf16[4,128,1024]{2,1,0:T(8,128)(2,1)S(1)}, bf16[4,128,1024]{2,1,0:T(8,128)(2,1)}, u32[]{:S(2)}, u32[]{:S(2)}) collective-permute-start(bf16[4,128,1024]{2,1,0:T(8,128)(2,1)S(1)} %all_to_all.10.left_any), channel_id=1, source_target_pairs={{0,1},{1,0},{2,3},{3,2},{4,5},{5,4},{6,7},{7,6},{8,9},{9,8},{10,11... | collective-permute-start | bytes 3145736 | tf_op jit(solution)/shard_map/ppermute | solution.py:321
  67.7 18.6 %collective-permute-start.1 = (bf16[64,1024]{1,0:T(8,128)(2,1)S(1)}, bf16[64,1024]{1,0:T(8,128)(2,1)S(1)}, u32[]{:S(2)}, u32[]{:S(2)}) collective-permute-start(bf16[64,1024]{1,0:T(8,128)(2,1)S(1)} %copy-done.1), channel_id=1, source_target_pairs={{0,512},{128,640},{256,768},{384,896},{512,0},{640,128},{768,256},... | collective-permute-start | bytes 393224 | tf_op jit(solution)/shard_map/ppermute | solution.py:321
  87.3 14.2 %collective-permute-start.3 = (bf16[128,1024]{1,0:T(8,128)(2,1)S(1)}, bf16[128,1024]{1,0:T(8,128)(2,1)S(1)}, u32[]{:S(2)}, u32[]{:S(2)}) collective-permute-start(bf16[128,1024]{1,0:T(8,128)(2,1)S(1)} %join.1), channel_id=1, source_target_pairs={{0,256},{128,384},{256,0},{384,128},{512,768},{640,896},{768,512},... | collective-permute-start | bytes 786440 | tf_op jit(solution)/shard_map/ppermute | solution.py:321
  89.2 15.6 %collective-permute-start.2 = (bf16[128,1024]{1,0:T(8,128)(2,1)S(1)}, bf16[128,1024]{1,0:T(8,128)(2,1)S(1)}, u32[]{:S(2)}, u32[]{:S(2)}) collective-permute-start(bf16[128,1024]{1,0:T(8,128)(2,1)S(1)} %join.1), channel_id=1, source_target_pairs={{0,128},{128,0},{256,384},{384,256},{512,640},{640,512},{768,896},... | collective-permute-start | bytes 786440 | tf_op jit(solution)/shard_map/ppermute | solution.py:321
  102.9 9.4 %copy-start = (s32[2,1]{0,1:T(1,128)S(1)}, s32[2,1]{0,1:T(1,128)}, u32[]{:S(2)}) copy-start(s32[2,1]{0,1:T(1,128)} %param.9) | copy-start | bytes 28
  102.9 9.4 %collective-permute-start.4 = (bf16[128,1024]{1,0:T(8,128)(2,1)}, bf16[128,1024]{1,0:T(8,128)(2,1)S(1)}, u32[]{:S(2)}, u32[]{:S(2)}) collective-permute-start(bf16[128,1024]{1,0:T(8,128)(2,1)} %bitcast.12), channel_id=1, source_target_pairs={{0,128},{128,0},{256,384},{384,256},{512,640},{640,512},{768,896},... | collective-permute-start | bytes 786440 | tf_op jit(solution)/shard_map/ppermute | solution.py:321
